TPU v7x, 256 devices: a whole 4x4x8 slice. The times are simulated.
256 devices in a mesh: gx: 4 (over y_lo, core), gy: 8 (over y_hi, x), gz: 8 (over z).
Axes of the slice: x: 4, y: 4 (y_hi: 2, y_lo: 2; y = y_hi * 2 + y_lo), z: 8, core: 2. Of those that a mesh axis runs over, the one named last changes fastest.
Arguments:
- positions: float32 [4, 8, 8, 3, 1024], P('gx', 'gy', 'gz'), may hold values from 0 to 1
- types: int32 [4, 8, 8, 1024], P('gx', 'gy', 'gz'), may hold values from 0 to 3
- tile_lists: int32 [8, 36], replicated, may hold values from 0 to 215, as said below
- hardness: float32 [4], replicated, may hold values from 2 to 8
- electroneg: float32 [4], replicated, may hold values from 2 to 8
- gamma_table: float32 [4], replicated, may hold values from 0.25 to 1
Outputs:
- charges: float32 [4, 8, 8, 1024], P('gx', 'gy', 'gz')
- solutions: float32 [4, 8, 8, 2, 1024], P('gx', 'gy', 'gz')
Inputs may be any that keep to these rules, and one draw needn't show every extreme that they name: `tile_lists`: entry (t, o, u) stands in tile t's list as often as entry (u, 26 - o, t) stands in tile u's list; every offset o of 0 to 26 occurs; the lists are the same for every box.
All inputs are finite; a program needn't handle non-finite values.
Results may differ from a plain program's by a relative error of at most 0.0003.
Values sent between devices are 32-bit elements; how exact they have to be, the bound alone decides.
No kernel may reach another device: no remote copies, remote signals or barrier semaphores. Data moves between devices by JAX's collectives and lax.ppermute only.
A program may use at most 64 MiB of HBM per device.

v0:
```python
import jax
import jax.numpy as jnp
from jax import lax
from jax.sharding import Mesh
from jax.sharding import PartitionSpec as P

ITERS = 4
GX_GY_GZ = ("gx_0", "gx_1", "gy_0", "gy_1", "gz")
GX = ("gx_0", "gx_1")
GY = ("gy_0", "gy_1")


CUTOFF = 10.0
COULOMB = 0.3
VOLUME = 10.0


def by_axis(shard, axes):
    for axis in axes:
        shard = lax.psum(shard, axis)
    return shard


def padded(cells, sides, width):
    for axis, dim in sides:
        count = lax.axis_size(axis)
        ends = count - 1
        head = lax.slice_in_dim(cells, 0, width, axis=dim)
        tail = lax.slice_in_dim(cells, cells.shape[dim] - width, cells.shape[dim], axis=dim)
        cells = jnp.concatenate(
            [
                lax.ppermute(tail, axis, [(i, (i + 1) % count) for i in range(ends)]),
                cells,
                lax.ppermute(head, axis, [((i + 1) % count, i) for i in range(ends)]),
            ],
            axis=dim,
        )
    return cells


def taper(scaled):
    return scaled**4 * (((20.0 * scaled - 70.0) * scaled + 84.0) * scaled - 35.0) + 1.0


def atom_table(types, table):
    kinds = jnp.arange(table.shape[0], dtype=jnp.int32)
    onehot = (types[..., None] == kinds).astype(jnp.float32)
    return jnp.dot(onehot, table, precision=lax.Precision.HIGHEST)


def arrange(raw, tile_count):
    channels = raw.shape[3]
    tile_width = raw.shape[4] // tile_count
    arranged = jnp.transpose(raw.reshape(27, channels, tile_count, tile_width), (1, 0, 2, 3))
    return arranged.reshape(channels, 27 * tile_count, tile_width)


def tile_blocks(nearby, tile_lists, box_edge):
    tile_count = tile_lists.shape[0]
    tile_width = nearby.shape[2]
    local_data = nearby[:, 13 * tile_count : 14 * tile_count]
    diagonal_mask = jnp.arange(tile_width)[:, None] == jnp.arange(tile_width)[None, :]

    def one_tile(inputs):
        mine_data, entries, tile_index = inputs
        others = nearby[:, entries]
        offset_box = entries // tile_count
        shifts = jnp.stack(
            [offset_box // 9 - 1, offset_box // 3 % 3 - 1, offset_box % 3 - 1]
        ).astype(jnp.float32)
        separation = (
            others[:3, :, None, :] + shifts[:, :, None, None] - mine_data[:3, None, :, None]
        ) * box_edge
        spacing = jnp.sqrt(jnp.sum(separation * separation, axis=0))
        present = others[4][:, None, :]
        gamma_other = others[3] + (1.0 - others[4])
        inverse_cube = (mine_data[3][None, :, None] * gamma_other[:, None, :]) ** (-1.5)
        shielding = jnp.cbrt(spacing * spacing * spacing + inverse_cube)
        tapered = jnp.where(spacing < CUTOFF, taper(spacing / CUTOFF), 0.0)
        coupling = COULOMB * tapered / shielding * present
        itself = (entries == 13 * tile_count + tile_index)[:, None, None] & diagonal_mask[None]
        return jnp.where(itself, 0.0, coupling)

    mine_all = jnp.transpose(local_data, (1, 0, 2))
    return lax.map(one_tile, (mine_all, tile_lists, jnp.arange(tile_count, dtype=jnp.int32)))


def couple(blocks, nearby_vectors, tile_lists):
    picked = nearby_vectors[:, tile_lists]
    return jnp.einsum("teij,ktej->kti", blocks, picked, precision=lax.Precision.HIGHEST)


def two_products(residual, image):
    return (
        by_axis(jnp.sum(residual * residual, axis=1), GX_GY_GZ),
        by_axis(jnp.sum(residual * image, axis=1), GX_GY_GZ),
    )


def on_device(positions, types, tile_lists, hardness, electroneg, gamma_table):
    atoms = positions.shape[4]
    tile_count = tile_lists.shape[0]
    box_edge = (atoms * VOLUME) ** (1.0 / 3.0)
    kinds = types[0, 0, 0]
    hardness_atom = atom_table(kinds, hardness)
    electro_atom = atom_table(kinds, electroneg)
    gamma_atom = atom_table(kinds, gamma_table)
    present = jnp.ones_like(gamma_atom)
    centre = jnp.concatenate([positions[0, 0, 0], gamma_atom[None], present[None]], axis=0)[
        None, None, None
    ]
    ghost_raw = padded(centre, ((GX, 0), (GY, 1), ("gz", 2)), 1)
    blocks = tile_blocks(arrange(ghost_raw, tile_count), tile_lists, box_edge)

    def apply(vectors):
        systems = vectors.shape[0]
        halo_raw = padded(vectors[None, None, None], ((GX, 0), (GY, 1), ("gz", 2)), 1)
        coupled = couple(blocks, arrange(halo_raw, tile_count), tile_lists).reshape(systems, atoms)
        return hardness_atom[None] * vectors + coupled

    right = jnp.stack([-electro_atom, -jnp.ones_like(electro_atom)], axis=0)
    solution = jnp.zeros_like(right)
    residual = right
    image = apply(residual)
    norm_now, product = two_products(residual, image)
    alpha = norm_now / product
    direction = residual
    along = image
    for iteration in range(ITERS):
        solution = solution + alpha[:, None] * direction
        residual = residual - alpha[:, None] * along
        if iteration + 1 < ITERS:
            image = apply(residual)
            norm_next, product = two_products(residual, image)
            ratio = norm_next / norm_now
            alpha = norm_next / (product - ratio * norm_next / alpha)
            direction = residual + ratio[:, None] * direction
            along = image + ratio[:, None] * along
            norm_now = norm_next
    sums = by_axis(jnp.sum(solution, axis=1), GX_GY_GZ)
    charges = solution[0] - sums[0] / sums[1] * solution[1]
    return (charges[None, None, None], solution[None, None, None])


def solution(mesh):
    split = Mesh(
        mesh.devices.reshape(2, 2, 2, 4, mesh.shape["gz"]), ("gx_0", "gx_1", "gy_0", "gy_1", "gz")
    )
    return jax.shard_map(
        on_device,
        mesh=split,
        in_specs=(P(GX, GY, "gz", None, None), P(GX, GY, "gz", None), P(), P(), P(), P()),
        out_specs=(P(GX, GY, "gz", None), P(GX, GY, "gz", None, None)),
        check_vma=False,
    )
```

profile of v0, /device:TPU:16, one launch (start us, length us, event | category | flops | bytes accessed | tf_op | source)
XLA Modules:
  0.0 517.7 jit_solution(2004003152165973501)
XLA Ops:
  18.7 6.1 %collective-permute-start.3 = (f32[3,1,1,2,1024]{4,3,2,1,0:T(2,128)S(1)}, f32[3,1,1,2,1024]{4,3,2,1,0:T(2,128)S(1)}, u32[]{:S(2)}, u32[]{:S(2)}) collective-permute-start(f32[3,1,1,2,1024]{4,3,2,1,0:T(2,128)S(1)} %pad_maximum_fusion.11), channel_id=1, source_target_pairs={{8,0},{16,8},{24,16},{32,24},{40,32},{48,40},{56,48},{9,1},{17,9},... | collective-permute-start | bytes 73736 | tf_op jit(solution)/shard_map/ppermute | solution.py:34
  26.7 7.5 %collective-permute-start.9 = (f32[3,1,1,5,1024]{4,3,2,1,0:T(8,128)S(1)}, f32[3,1,1,5,1024]{4,3,2,1,0:T(8,128)S(1)}, u32[]{:S(2)}, u32[]{:S(2)}) collective-permute-start(f32[3,1,1,5,1024]{4,3,2,1,0:T(8,128)S(1)} %pad_maximum_fusion.6), channel_id=1, source_target_pairs={{8,0},{16,8},{24,16},{32,24},{40,32},{48,40},{56,48},{9,1},{17,9},... | collective-permute-start | bytes 184328 | tf_op jit(solution)/shard_map/ppermute | solution.py:34
  56.2 93.0 %while.14 = (s32[]{:T(128)}, f32[8,36,128,128]{3,2,1,0:T(8,128)}, s32[8,36]{1,0:T(8,128)}, s32[8]{0:T(128)S(1)}, f32[5,216,128]{2,0,1:T(8,128)S(1)}, /*index=5*/f32[8,5,128]{2,1,0:T(8,128)S(1)}, s32[]{:T(128)}, s32[1]{0:T(128)}) while((s32[]{:T(128)}, f32[8,36,128,128]{3,2,1,0:T(8,128)}, s32[8,36]{1,0:T(8,128)}, s32[8]{0:T(128)S(1)}, ...), condition=%wide.region_8.9_spmd.clone, body=%wide.region_6.8_spmd.clone.sunk | while | flops 19506696 | bytes 7794025 | solution.py:85
  61.7 6.1 %fusion.74 = f32[8,36,128,128]{3,2,1,0:T(8,128)} fusion(f32[8,36,128,128]{3,2,1,0:T(8,128)} %get-tuple-element.309, s32[]{:T(128)} %get-tuple-element.308, f32[36,128,128]{2,1,0:T(8,128)S(1)} %multiply_reduce_fusion.7, f32[36,128]{1,0:T(8,128)S(1)} %bitcast.196, f32[36,128]{1,0:T(8,128)S(1)} %bitcast_add_fusion.2, f32[128]{0:T(128)S(1)} %slice_bitcast_fusion.6, ...), kind=kLoop, calls=%fused_computation.13.clone.1 | loop fusion | flops 12976128 | bytes 4772900 | tf_op jit(solution)/shard_map/while/body/jit(dynamic_update_index_in_dim)/dynamic_update_slice | solution.py:85
  73.4 6.1 %fusion.74 = f32[8,36,128,128]{3,2,1,0:T(8,128)} fusion(f32[8,36,128,128]{3,2,1,0:T(8,128)} %get-tuple-element.309, s32[]{:T(128)} %get-tuple-element.308, f32[36,128,128]{2,1,0:T(8,128)S(1)} %multiply_reduce_fusion.7, f32[36,128]{1,0:T(8,128)S(1)} %bitcast.196, f32[36,128]{1,0:T(8,128)S(1)} %bitcast_add_fusion.2, f32[128]{0:T(128)S(1)} %slice_bitcast_fusion.6, ...), kind=kLoop, calls=%fused_computation.13.clone.1 | loop fusion | flops 12976128 | bytes 4772900 | tf_op jit(solution)/shard_map/while/body/jit(dynamic_update_index_in_dim)/dynamic_update_slice | solution.py:85
  84.9 6.1 %fusion.74 = f32[8,36,128,128]{3,2,1,0:T(8,128)} fusion(f32[8,36,128,128]{3,2,1,0:T(8,128)} %get-tuple-element.309, s32[]{:T(128)} %get-tuple-element.308, f32[36,128,128]{2,1,0:T(8,128)S(1)} %multiply_reduce_fusion.7, f32[36,128]{1,0:T(8,128)S(1)} %bitcast.196, f32[36,128]{1,0:T(8,128)S(1)} %bitcast_add_fusion.2, f32[128]{0:T(128)S(1)} %slice_bitcast_fusion.6, ...), kind=kLoop, calls=%fused_computation.13.clone.1 | loop fusion | flops 12976128 | bytes 4772900 | tf_op jit(solution)/shard_map/while/body/jit(dynamic_update_index_in_dim)/dynamic_update_slice | solution.py:85
  96.5 6.2 %fusion.74 = f32[8,36,128,128]{3,2,1,0:T(8,128)} fusion(f32[8,36,128,128]{3,2,1,0:T(8,128)} %get-tuple-element.309, s32[]{:T(128)} %get-tuple-element.308, f32[36,128,128]{2,1,0:T(8,128)S(1)} %multiply_reduce_fusion.7, f32[36,128]{1,0:T(8,128)S(1)} %bitcast.196, f32[36,128]{1,0:T(8,128)S(1)} %bitcast_add_fusion.2, f32[128]{0:T(128)S(1)} %slice_bitcast_fusion.6, ...), kind=kLoop, calls=%fused_computation.13.clone.1 | loop fusion | flops 12976128 | bytes 4772900 | tf_op jit(solution)/shard_map/while/body/jit(dynamic_update_index_in_dim)/dynamic_update_slice | solution.py:85
  108.2 6.1 %fusion.74 = f32[8,36,128,128]{3,2,1,0:T(8,128)} fusion(f32[8,36,128,128]{3,2,1,0:T(8,128)} %get-tuple-element.309, s32[]{:T(128)} %get-tuple-element.308, f32[36,128,128]{2,1,0:T(8,128)S(1)} %multiply_reduce_fusion.7, f32[36,128]{1,0:T(8,128)S(1)} %bitcast.196, f32[36,128]{1,0:T(8,128)S(1)} %bitcast_add_fusion.2, f32[128]{0:T(128)S(1)} %slice_bitcast_fusion.6, ...), kind=kLoop, calls=%fused_computation.13.clone.1 | loop fusion | flops 12976128 | bytes 4772900 | tf_op jit(solution)/shard_map/while/body/jit(dynamic_update_index_in_dim)/dynamic_update_slice | solution.py:85
  119.8 6.1 %fusion.74 = f32[8,36,128,128]{3,2,1,0:T(8,128)} fusion(f32[8,36,128,128]{3,2,1,0:T(8,128)} %get-tuple-element.309, s32[]{:T(128)} %get-tuple-element.308, f32[36,128,128]{2,1,0:T(8,128)S(1)} %multiply_reduce_fusion.7, f32[36,128]{1,0:T(8,128)S(1)} %bitcast.196, f32[36,128]{1,0:T(8,128)S(1)} %bitcast_add_fusion.2, f32[128]{0:T(128)S(1)} %slice_bitcast_fusion.6, ...), kind=kLoop, calls=%fused_computation.13.clone.1 | loop fusion | flops 12976128 | bytes 4772900 | tf_op jit(solution)/shard_map/while/body/jit(dynamic_update_index_in_dim)/dynamic_update_slice | solution.py:85
  131.4 6.1 %fusion.74 = f32[8,36,128,128]{3,2,1,0:T(8,128)} fusion(f32[8,36,128,128]{3,2,1,0:T(8,128)} %get-tuple-element.309, s32[]{:T(128)} %get-tuple-element.308, f32[36,128,128]{2,1,0:T(8,128)S(1)} %multiply_reduce_fusion.7, f32[36,128]{1,0:T(8,128)S(1)} %bitcast.196, f32[36,128]{1,0:T(8,128)S(1)} %bitcast_add_fusion.2, f32[128]{0:T(128)S(1)} %slice_bitcast_fusion.6, ...), kind=kLoop, calls=%fused_computation.13.clone.1 | loop fusion | flops 12976128 | bytes 4772900 | tf_op jit(solution)/shard_map/while/body/jit(dynamic_update_index_in_dim)/dynamic_update_slice | solution.py:85
  143.1 6.2 %fusion.74 = f32[8,36,128,128]{3,2,1,0:T(8,128)} fusion(f32[8,36,128,128]{3,2,1,0:T(8,128)} %get-tuple-element.309, s32[]{:T(128)} %get-tuple-element.308, f32[36,128,128]{2,1,0:T(8,128)S(1)} %multiply_reduce_fusion.7, f32[36,128]{1,0:T(8,128)S(1)} %bitcast.196, f32[36,128]{1,0:T(8,128)S(1)} %bitcast_add_fusion.2, f32[128]{0:T(128)S(1)} %slice_bitcast_fusion.6, ...), kind=kLoop, calls=%fused_computation.13.clone.1 | loop fusion | flops 12976128 | bytes 4772900 | tf_op jit(solution)/shard_map/while/body/jit(dynamic_update_index_in_dim)/dynamic_update_slice | solution.py:85
  149.2 18.6 %fusion.36 = (f32[2]{0:T(128)S(1)}, f32[2]{0:T(128)S(1)}, f32[2,1024]{1,0:T(2,128)S(1)}) fusion(f32[1,1024]{1,0:T(1,128)S(1)} %bitcast.216, f32[2,8,36,128]{3,0,2,1:T(2,128)S(1)} %bitcast.197, f32[8,36,128,128]{3,2,1,0:T(8,128)} %get-tuple-element.137, f32[1024]{0:T(1024)S(1)} %bitcast.201), kind=kOutput, calls=%fused_computation.101 | convolution fusion | flops 113258496 | bytes 19185680 | tf_op jit(solution)/shard_map/teij,ktej->kti/dot_general | solution.py:90
  175.2 6.4 %all-reduce.12 = (f32[2]{0:T(128)S(1)}, f32[2]{0:T(128)S(1)}) all-reduce(f32[2]{0:T(128)S(1)} %get-tuple-element.218, f32[2]{0:T(128)S(1)} %get-tuple-element.219), channel_id=1, replica_groups=mesh['gx_0'=2,'gx_1'=2,'gy_0'=2,'gy_1'=4,'gz'=8] {'gy_0'}, use_global_device_ids=true, to_apply=%region_3.4 | all-reduce | flops 4 | bytes 32 | tf_op jit(solution)/shard_map/psum | solution.py:20
  181.6 7.7 %all-reduce.8 = (f32[2]{0:T(128)S(1)}, f32[2]{0:T(128)S(1)}) all-reduce(f32[2]{0:T(128)S(1)} %get-tuple-element.210, f32[2]{0:T(128)S(1)} %get-tuple-element.211), channel_id=1, replica_groups=mesh['gx_0'=2,'gx_1'=2,'gy_0'=2,'gy_1'=4,'gz'=8] {'gy_1'}, use_global_device_ids=true, to_apply=%region_4.5 | all-reduce | flops 4 | bytes 32 | tf_op jit(solution)/shard_map/psum | solution.py:20
  189.3 19.9 %all-reduce.4 = (f32[2]{0:T(128)S(1)}, f32[2]{0:T(128)S(1)}) all-reduce(f32[2]{0:T(128)S(1)} %get-tuple-element.202, f32[2]{0:T(128)S(1)} %get-tuple-element.203), channel_id=1, replica_groups=mesh['gx_0'=2,'gx_1'=2,'gy_0'=2,'gy_1'=4,'gz'=8] {'gz'}, use_global_device_ids=true, to_apply=%region_5.6 | all-reduce | flops 4 | bytes 32 | tf_op jit(solution)/shard_map/psum | solution.py:20
  236.5 18.6 %multiply_reduce_fusion.4 = (f32[2]{0:T(128)S(1)}, f32[2]{0:T(128)S(1)}, f32[2,1024]{1,0:T(2,128)S(1)}) fusion(f32[2,8,36,128]{3,0,2,1:T(2,128)S(1)} %bitcast.198, f32[8,36,128,128]{3,2,1,0:T(8,128)} %get-tuple-element.137, f32[1024]{0:T(1024)S(1)} %bitcast.202, f32[2,1024]{1,0:T(2,128)S(1)} %get-tuple-element.248, f32[2]{0:T(128)S(1)} %div.83, ...), kind=kOutput, calls=%fused_computation.112 | convolution fusion | flops 113262592 | bytes 19193880 | tf_op jit(solution)/shard_map/teij,ktej->kti/dot_general | solution.py:90
  262.5 6.4 %all-reduce.11 = (f32[2]{0:T(128)S(1)}, f32[2]{0:T(128)S(1)}) all-reduce(f32[2]{0:T(128)S(1)} %get-tuple-element.216, f32[2]{0:T(128)S(1)} %get-tuple-element.217), channel_id=1, replica_groups=mesh['gx_0'=2,'gx_1'=2,'gy_0'=2,'gy_1'=4,'gz'=8] {'gy_0'}, use_global_device_ids=true, to_apply=%region_18.19 | all-reduce | flops 4 | bytes 32 | tf_op jit(solution)/shard_map/psum | solution.py:20
  268.9 10.9 %all-reduce.7 = (f32[2]{0:T(128)S(1)}, f32[2]{0:T(128)S(1)}) all-reduce(f32[2]{0:T(128)S(1)} %get-tuple-element.208, f32[2]{0:T(128)S(1)} %get-tuple-element.209), channel_id=1, replica_groups=mesh['gx_0'=2,'gx_1'=2,'gy_0'=2,'gy_1'=4,'gz'=8] {'gy_1'}, use_global_device_ids=true, to_apply=%region_19.20 | all-reduce | flops 4 | bytes 32 | tf_op jit(solution)/shard_map/psum | solution.py:20
  279.8 18.3 %all-reduce.3 = (f32[2]{0:T(128)S(1)}, f32[2]{0:T(128)S(1)}) all-reduce(f32[2]{0:T(128)S(1)} %get-tuple-element.200, f32[2]{0:T(128)S(1)} %get-tuple-element.201), channel_id=1, replica_groups=mesh['gx_0'=2,'gx_1'=2,'gy_0'=2,'gy_1'=4,'gz'=8] {'gz'}, use_global_device_ids=true, to_apply=%region_20.21 | all-reduce | flops 4 | bytes 32 | tf_op jit(solution)/shard_map/psum | solution.py:20
  306.6 7.5 %collective-permute-start.21 = (f32[3,1,1,2,1024]{4,3,2,1,0:T(2,128)S(1)}, f32[3,1,1,2,1024]{4,3,2,1,0:T(2,128)S(1)}, u32[]{:S(2)}, u32[]{:S(2)}) collective-permute-start(f32[3,1,1,2,1024]{4,3,2,1,0:T(2,128)S(1)} %pad_maximum_fusion.13), channel_id=1, source_target_pairs={{8,0},{16,8},{24,16},{32,24},{40,32},{48,40},{56,48},{9,1},{17,9},... | collective-permute-start | bytes 73736 | tf_op jit(solution)/shard_map/ppermute | solution.py:34
  326.9 18.6 %multiply_reduce_fusion.2 = (f32[2]{0:T(128)S(1)}, f32[2]{0:T(128)S(1)}, f32[2,1024]{1,0:T(2,128)S(1)}) fusion(f32[2,1024]{1,0:T(2,128)S(1)} %multiply_subtract_fusion.1, f32[2,8,36,128]{3,0,2,1:T(2,128)S(1)} %bitcast.199, f32[8,36,128,128]{3,2,1,0:T(8,128)} %get-tuple-element.137, f32[1024]{0:T(1024)S(1)} %bitcast.203), kind=kOutput, calls=%fused_computation.108 | convolution fusion | flops 113258496 | bytes 19189776 | tf_op jit(solution)/shard_map/teij,ktej->kti/dot_general | solution.py:90
  352.9 6.6 %all-reduce.10 = (f32[2]{0:T(128)S(1)}, f32[2]{0:T(128)S(1)}) all-reduce(f32[2]{0:T(128)S(1)} %get-tuple-element.214, f32[2]{0:T(128)S(1)} %get-tuple-element.215), channel_id=1, replica_groups=mesh['gx_0'=2,'gx_1'=2,'gy_0'=2,'gy_1'=4,'gz'=8] {'gy_0'}, use_global_device_ids=true, to_apply=%region_30.31 | all-reduce | flops 4 | bytes 32 | tf_op jit(solution)/shard_map/psum | solution.py:20
  359.5 10.9 %all-reduce.6 = (f32[2]{0:T(128)S(1)}, f32[2]{0:T(128)S(1)}) all-reduce(f32[2]{0:T(128)S(1)} %get-tuple-element.206, f32[2]{0:T(128)S(1)} %get-tuple-element.207), channel_id=1, replica_groups=mesh['gx_0'=2,'gx_1'=2,'gy_0'=2,'gy_1'=4,'gz'=8] {'gy_1'}, use_global_device_ids=true, to_apply=%region_31.32 | all-reduce | flops 4 | bytes 32 | tf_op jit(solution)/shard_map/psum | solution.py:20
  370.5 18.3 %all-reduce.2 = (f32[2]{0:T(128)S(1)}, f32[2]{0:T(128)S(1)}) all-reduce(f32[2]{0:T(128)S(1)} %get-tuple-element.198, f32[2]{0:T(128)S(1)} %get-tuple-element.199), channel_id=1, replica_groups=mesh['gx_0'=2,'gx_1'=2,'gy_0'=2,'gy_1'=4,'gz'=8] {'gz'}, use_global_device_ids=true, to_apply=%region_32.33 | all-reduce | flops 4 | bytes 32 | tf_op jit(solution)/shard_map/psum | solution.py:20
  397.3 7.5 %collective-permute-start.27 = (f32[3,1,1,2,1024]{4,3,2,1,0:T(2,128)S(1)}, f32[3,1,1,2,1024]{4,3,2,1,0:T(2,128)S(1)}, u32[]{:S(2)}, u32[]{:S(2)}) collective-permute-start(f32[3,1,1,2,1024]{4,3,2,1,0:T(2,128)S(1)} %pad_maximum_fusion.14), channel_id=1, source_target_pairs={{8,0},{16,8},{24,16},{32,24},{40,32},{48,40},{56,48},{9,1},{17,9},... | collective-permute-start | bytes 73736 | tf_op jit(solution)/shard_map/ppermute | solution.py:34
  417.7 18.5 %fusion.28 = f32[2]{0:T(128)S(1)} fusion(f32[2,1024]{1,0:T(2,128)S(1)} %get-tuple-element.235, f32[2,8,36,128]{3,0,2,1:T(2,128)S(1)} %bitcast.200, f32[8,36,128,128]{3,2,1,0:T(8,128)} %get-tuple-element.137, f32[1024]{0:T(1024)S(1)} %bitcast.204), kind=kOutput, calls=%fused_computation.61 | convolution fusion | flops 113254400 | bytes 19181576 | tf_op jit(solution)/shard_map/teij,ktej->kti/dot_general | solution.py:90
  443.6 6.4 %all-reduce.9 = (f32[2]{0:T(128)S(1)}, f32[2]{0:T(128)S(1)}) all-reduce(f32[2]{0:T(128)S(1)} %get-tuple-element.212, f32[2]{0:T(128)S(1)} %get-tuple-element.213), channel_id=1, replica_groups=mesh['gx_0'=2,'gx_1'=2,'gy_0'=2,'gy_1'=4,'gz'=8] {'gy_0'}, use_global_device_ids=true, to_apply=%region_42.43 | all-reduce | flops 4 | bytes 32 | tf_op jit(solution)/shard_map/psum | solution.py:20
  450.0 10.9 %all-reduce.5 = (f32[2]{0:T(128)S(1)}, f32[2]{0:T(128)S(1)}) all-reduce(f32[2]{0:T(128)S(1)} %get-tuple-element.204, f32[2]{0:T(128)S(1)} %get-tuple-element.205), channel_id=1, replica_groups=mesh['gx_0'=2,'gx_1'=2,'gy_0'=2,'gy_1'=4,'gz'=8] {'gy_1'}, use_global_device_ids=true, to_apply=%region_43.44 | all-reduce | flops 4 | bytes 32 | tf_op jit(solution)/shard_map/psum | solution.py:20
  461.0 18.3 %all-reduce.1 = (f32[2]{0:T(128)S(1)}, f32[2]{0:T(128)S(1)}) all-reduce(f32[2]{0:T(128)S(1)} %get-tuple-element.196, f32[2]{0:T(128)S(1)} %get-tuple-element.197), channel_id=1, replica_groups=mesh['gx_0'=2,'gx_1'=2,'gy_0'=2,'gy_1'=4,'gz'=8] {'gz'}, use_global_device_ids=true, to_apply=%region_44.45 | all-reduce | flops 4 | bytes 32 | tf_op jit(solution)/shard_map/psum | solution.py:20
  486.9 6.4 %psum.357 = f32[2]{0:T(128)S(1)} all-reduce(f32[2]{0:T(128)S(1)} %psum.356), channel_id=1, replica_groups=mesh['gx_0'=2,'gx_1'=2,'gy_0'=2,'gy_1'=4,'gz'=8] {'gy_0'}, use_global_device_ids=true, to_apply=%region_54.55 | all-reduce | flops 2 | bytes 16 | tf_op jit(solution)/shard_map/psum | solution.py:20
  493.3 7.7 %psum.358 = f32[2]{0:T(128)S(1)} all-reduce(f32[2]{0:T(128)S(1)} %psum.357), channel_id=1, replica_groups=mesh['gx_0'=2,'gx_1'=2,'gy_0'=2,'gy_1'=4,'gz'=8] {'gy_1'}, use_global_device_ids=true, to_apply=%region_55.56 | all-reduce | flops 2 | bytes 16 | tf_op jit(solution)/shard_map/psum | solution.py:20
  501.0 14.1 %psum.359 = f32[2]{0:T(128)S(1)} all-reduce(f32[2]{0:T(128)S(1)} %psum.358), channel_id=1, replica_groups=mesh['gx_0'=2,'gx_1'=2,'gy_0'=2,'gy_1'=4,'gz'=8] {'gz'}, use_global_device_ids=true, to_apply=%region_56.57 | all-reduce | flops 2 | bytes 16 | tf_op jit(solution)/shard_map/psum | solution.py:20
  (280 shorter events, 187.7 us)
Async XLA Ops:
  0.6 0.7 copy-start
  2.7 22.1 %collective-permute-start.6 = (f32[1,1,1,5,1024]{4,3,2,1,0:T(8,128)S(1)}, f32[1,1,1,5,1024]{4,3,2,1,0:T(8,128)S(1)}, u32[]{:S(2)}, u32[]{:S(2)}) collective-permute-start(f32[1,1,1,5,1024]{4,3,2,1,0:T(8,128)S(1)} %maximum_bitcast_fusion), channel_id=1, source_target_pairs={{0,64},{64,128},{128,192},{1,65},{65,129},{129,193},{2,66},{66,130... | collective-permute-start | bytes 61448 | tf_op jit(solution)/shard_map/ppermute | solution.py:32
  4.4 20.4 %collective-permute-start.7 = (f32[1,1,1,5,1024]{4,3,2,1,0:T(8,128)S(1)}, f32[1,1,1,5,1024]{4,3,2,1,0:T(8,128)S(1)}, u32[]{:S(2)}, u32[]{:S(2)}) collective-permute-start(f32[1,1,1,5,1024]{4,3,2,1,0:T(8,128)S(1)} %maximum_bitcast_fusion), channel_id=1, source_target_pairs={{64,0},{128,64},{192,128},{65,1},{129,65},{193,129},{66,2},{130,66... | collective-permute-start | bytes 61448 | tf_op jit(solution)/shard_map/ppermute | solution.py:34
  6.9 7.4 %collective-permute-start = (f32[1,1,1,2,1024]{4,3,2,1,0:T(2,128)S(1)}, f32[1,1,1,2,1024]{4,3,2,1,0:T(2,128)S(1)}, u32[]{:S(2)}, u32[]{:S(2)}) collective-permute-start(f32[1,1,1,2,1024]{4,3,2,1,0:T(2,128)S(1)} %pad_bitcast_fusion), channel_id=1, source_target_pairs={{0,64},{64,128},{128,192},{1,65},{65,129},{129,193},{2,66},{66,130... | collective-permute-start | bytes 24584 | tf_op jit(solution)/shard_map/ppermute | solution.py:32
  11.0 4.3 collective-permute-start.1
  15.3 19.0 %collective-permute-start.2 = (f32[3,1,1,2,1024]{4,3,2,1,0:T(2,128)S(1)}, f32[3,1,1,2,1024]{4,3,2,1,0:T(2,128)S(1)}, u32[]{:S(2)}, u32[]{:S(2)}) collective-permute-start(f32[3,1,1,2,1024]{4,3,2,1,0:T(2,128)S(1)} %pad_maximum_fusion.11), channel_id=1, source_target_pairs={{0,8},{8,16},{16,24},{24,32},{32,40},{40,48},{48,56},{1,9},{9,17},... | collective-permute-start | bytes 73736 | tf_op jit(solution)/shard_map/ppermute | solution.py:32
  18.7 15.6 %collective-permute-start.3 = (f32[3,1,1,2,1024]{4,3,2,1,0:T(2,128)S(1)}, f32[3,1,1,2,1024]{4,3,2,1,0:T(2,128)S(1)}, u32[]{:S(2)}, u32[]{:S(2)}) collective-permute-start(f32[3,1,1,2,1024]{4,3,2,1,0:T(2,128)S(1)} %pad_maximum_fusion.11), channel_id=1, source_target_pairs={{8,0},{16,8},{24,16},{32,24},{40,32},{48,40},{56,48},{9,1},{17,9},... | collective-permute-start | bytes 73736 | tf_op jit(solution)/shard_map/ppermute | solution.py:34
  24.8 14.7 %collective-permute-start.8 = (f32[3,1,1,5,1024]{4,3,2,1,0:T(8,128)S(1)}, f32[3,1,1,5,1024]{4,3,2,1,0:T(8,128)S(1)}, u32[]{:S(2)}, u32[]{:S(2)}) collective-permute-start(f32[3,1,1,5,1024]{4,3,2,1,0:T(8,128)S(1)} %pad_maximum_fusion.6), channel_id=1, source_target_pairs={{0,8},{8,16},{16,24},{24,32},{32,40},{40,48},{48,56},{1,9},{9,17},... | collective-permute-start | bytes 184328 | tf_op jit(solution)/shard_map/ppermute | solution.py:32
  26.7 12.8 %collective-permute-start.9 = (f32[3,1,1,5,1024]{4,3,2,1,0:T(8,128)S(1)}, f32[3,1,1,5,1024]{4,3,2,1,0:T(8,128)S(1)}, u32[]{:S(2)}, u32[]{:S(2)}) collective-permute-start(f32[3,1,1,5,1024]{4,3,2,1,0:T(8,128)S(1)} %pad_maximum_fusion.6), channel_id=1, source_target_pairs={{8,0},{16,8},{24,16},{32,24},{40,32},{48,40},{56,48},{9,1},{17,9},... | collective-permute-start | bytes 184328 | tf_op jit(solution)/shard_map/ppermute | solution.py:34
  34.3 11.1 %collective-permute-start.4 = (f32[3,3,1,2,1024]{4,3,2,1,0:T(2,128)S(1)}, f32[3,3,1,2,1024]{4,3,2,1,0:T(2,128)S(1)}, u32[]{:S(2)}, u32[]{:S(2)}) collective-permute-start(f32[3,3,1,2,1024]{4,3,2,1,0:T(2,128)S(1)} %pad_maximum_fusion.7), channel_id=1, source_target_pairs={{0,1},{1,2},{2,3},{3,4},{4,5},{5,6},{6,7},{8,9},{9,10},{10,11},{11... | collective-permute-start | bytes 221192 | tf_op jit(solution)/shard_map/ppermute | solution.py:32
  38.2 7.2 %collective-permute-start.5 = (f32[3,3,1,2,1024]{4,3,2,1,0:T(2,128)S(1)}, f32[3,3,1,2,1024]{4,3,2,1,0:T(2,128)S(1)}, u32[]{:S(2)}, u32[]{:S(2)}) collective-permute-start(f32[3,3,1,2,1024]{4,3,2,1,0:T(2,128)S(1)} %pad_maximum_fusion.7), channel_id=1, source_target_pairs={{1,0},{2,1},{3,2},{4,3},{5,4},{6,5},{7,6},{9,8},{10,9},{11,10},{12... | collective-permute-start | bytes 221192 | tf_op jit(solution)/shard_map/ppermute | solution.py:34
  39.5 11.9 %collective-permute-start.10 = (f32[3,3,1,5,1024]{4,3,2,1,0:T(8,128)S(1)}, f32[3,3,1,5,1024]{4,3,2,1,0:T(8,128)S(1)}, u32[]{:S(2)}, u32[]{:S(2)}) collective-permute-start(f32[3,3,1,5,1024]{4,3,2,1,0:T(8,128)S(1)} %pad_maximum_fusion.1), channel_id=1, source_target_pairs={{0,1},{1,2},{2,3},{3,4},{4,5},{5,6},{6,7},{8,9},{9,10},{10,11},{11... | collective-permute-start | bytes 552968 | tf_op jit(solution)/shard_map/ppermute | solution.py:32
  44.1 11.6 %collective-permute-start.11 = (f32[3,3,1,5,1024]{4,3,2,1,0:T(8,128)S(1)}, f32[3,3,1,5,1024]{4,3,2,1,0:T(8,128)S(1)}, u32[]{:S(2)}, u32[]{:S(2)}) collective-permute-start(f32[3,3,1,5,1024]{4,3,2,1,0:T(8,128)S(1)} %pad_maximum_fusion.1), channel_id=1, source_target_pairs={{1,0},{2,1},{3,2},{4,3},{5,4},{6,5},{7,6},{9,8},{10,9},{11,10},{12... | collective-permute-start | bytes 552968 | tf_op jit(solution)/shard_map/ppermute | solution.py:34
  209.3 2.6 collective-permute-start.12
  210.6 3.6 collective-permute-start.13
  214.2 9.5 %collective-permute-start.14 = (f32[3,1,1,2,1024]{4,3,2,1,0:T(2,128)S(1)}, f32[3,1,1,2,1024]{4,3,2,1,0:T(2,128)S(1)}, u32[]{:S(2)}, u32[]{:S(2)}) collective-permute-start(f32[3,1,1,2,1024]{4,3,2,1,0:T(2,128)S(1)} %pad_maximum_fusion.12), channel_id=1, source_target_pairs={{0,8},{8,16},{16,24},{24,32},{32,40},{40,48},{48,56},{1,9},{9,17},... | collective-permute-start | bytes 73736 | tf_op jit(solution)/shard_map/ppermute | solution.py:32
  218.2 7.0 %collective-permute-start.15 = (f32[3,1,1,2,1024]{4,3,2,1,0:T(2,128)S(1)}, f32[3,1,1,2,1024]{4,3,2,1,0:T(2,128)S(1)}, u32[]{:S(2)}, u32[]{:S(2)}) collective-permute-start(f32[3,1,1,2,1024]{4,3,2,1,0:T(2,128)S(1)} %pad_maximum_fusion.12), channel_id=1, source_target_pairs={{8,0},{16,8},{24,16},{32,24},{40,32},{48,40},{56,48},{9,1},{17,9},... | collective-permute-start | bytes 73736 | tf_op jit(solution)/shard_map/ppermute | solution.py:34
  225.2 4.0 collective-permute-start.16
  226.9 7.0 %collective-permute-start.17 = (f32[3,3,1,2,1024]{4,3,2,1,0:T(2,128)S(1)}, f32[3,3,1,2,1024]{4,3,2,1,0:T(2,128)S(1)}, u32[]{:S(2)}, u32[]{:S(2)}) collective-permute-start(f32[3,3,1,2,1024]{4,3,2,1,0:T(2,128)S(1)} %pad_maximum_fusion.8), channel_id=1, source_target_pairs={{1,0},{2,1},{3,2},{4,3},{5,4},{6,5},{7,6},{9,8},{10,9},{11,10},{12... | collective-permute-start | bytes 221192 | tf_op jit(solution)/shard_map/ppermute | solution.py:34
  298.2 2.6 collective-permute-start.18
  299.5 5.1 collective-permute-start.19
  304.7 9.5 %collective-permute-start.20 = (f32[3,1,1,2,1024]{4,3,2,1,0:T(2,128)S(1)}, f32[3,1,1,2,1024]{4,3,2,1,0:T(2,128)S(1)}, u32[]{:S(2)}, u32[]{:S(2)}) collective-permute-start(f32[3,1,1,2,1024]{4,3,2,1,0:T(2,128)S(1)} %pad_maximum_fusion.13), channel_id=1, source_target_pairs={{0,8},{8,16},{16,24},{24,32},{32,40},{40,48},{48,56},{1,9},{9,17},... | collective-permute-start | bytes 73736 | tf_op jit(solution)/shard_map/ppermute | solution.py:32
  306.6 9.0 %collective-permute-start.21 = (f32[3,1,1,2,1024]{4,3,2,1,0:T(2,128)S(1)}, f32[3,1,1,2,1024]{4,3,2,1,0:T(2,128)S(1)}, u32[]{:S(2)}, u32[]{:S(2)}) collective-permute-start(f32[3,1,1,2,1024]{4,3,2,1,0:T(2,128)S(1)} %pad_maximum_fusion.13), channel_id=1, source_target_pairs={{8,0},{16,8},{24,16},{32,24},{40,32},{48,40},{56,48},{9,1},{17,9},... | collective-permute-start | bytes 73736 | tf_op jit(solution)/shard_map/ppermute | solution.py:34
  315.7 4.0 collective-permute-start.22
  317.3 7.0 %collective-permute-start.23 = (f32[3,3,1,2,1024]{4,3,2,1,0:T(2,128)S(1)}, f32[3,3,1,2,1024]{4,3,2,1,0:T(2,128)S(1)}, u32[]{:S(2)}, u32[]{:S(2)}) collective-permute-start(f32[3,3,1,2,1024]{4,3,2,1,0:T(2,128)S(1)} %pad_maximum_fusion.9), channel_id=1, source_target_pairs={{1,0},{2,1},{3,2},{4,3},{5,4},{6,5},{7,6},{9,8},{10,9},{11,10},{12... | collective-permute-start | bytes 221192 | tf_op jit(solution)/shard_map/ppermute | solution.py:34
  389.0 2.6 collective-permute-start.24
  390.3 5.1 collective-permute-start.25
  395.4 9.5 %collective-permute-start.26 = (f32[3,1,1,2,1024]{4,3,2,1,0:T(2,128)S(1)}, f32[3,1,1,2,1024]{4,3,2,1,0:T(2,128)S(1)}, u32[]{:S(2)}, u32[]{:S(2)}) collective-permute-start(f32[3,1,1,2,1024]{4,3,2,1,0:T(2,128)S(1)} %pad_maximum_fusion.14), channel_id=1, source_target_pairs={{0,8},{8,16},{16,24},{24,32},{32,40},{40,48},{48,56},{1,9},{9,17},... | collective-permute-start | bytes 73736 | tf_op jit(solution)/shard_map/ppermute | solution.py:32
  397.3 9.0 %collective-permute-start.27 = (f32[3,1,1,2,1024]{4,3,2,1,0:T(2,128)S(1)}, f32[3,1,1,2,1024]{4,3,2,1,0:T(2,128)S(1)}, u32[]{:S(2)}, u32[]{:S(2)}) collective-permute-start(f32[3,1,1,2,1024]{4,3,2,1,0:T(2,128)S(1)} %pad_maximum_fusion.14), channel_id=1, source_target_pairs={{8,0},{16,8},{24,16},{32,24},{40,32},{48,40},{56,48},{9,1},{17,9},... | collective-permute-start | bytes 73736 | tf_op jit(solution)/shard_map/ppermute | solution.py:34
  406.4 4.0 collective-permute-start.28
  408.1 7.0 %collective-permute-start.29 = (f32[3,3,1,2,1024]{4,3,2,1,0:T(2,128)S(1)}, f32[3,3,1,2,1024]{4,3,2,1,0:T(2,128)S(1)}, u32[]{:S(2)}, u32[]{:S(2)}) collective-permute-start(f32[3,3,1,2,1024]{4,3,2,1,0:T(2,128)S(1)} %pad_maximum_fusion.10), channel_id=1, source_target_pairs={{1,0},{2,1},{3,2},{4,3},{5,4},{6,5},{7,6},{9,8},{10,9},{11,10},{12... | collective-permute-start | bytes 221192 | tf_op jit(solution)/shard_map/ppermute | solution.py:34
  479.5 38.2 %copy-start.1 = (f32[2,1024]{1,0:T(2,128)}, f32[2,1024]{1,0:T(2,128)S(1)}, u32[]{:S(2)}) copy-start(f32[2,1024]{1,0:T(2,128)S(1)} %get-tuple-element.231) | copy-start | bytes 24580
where the time goes:
time: 524 us; the launch traced here: 518 us
  blocking collectives  206 us (39%)
  starting transfers between devices  83.4 us (16%)
  other arithmetic  79.2 us (15%)
  matrix products  77.7 us (15%)
  waiting for transfers between devices  40.1 us (8%)
  local copies, waits for them, and re-layouts  22.4 us (4%)
  loops' own time  5.87 us (1%)
    psum x25, blocking collectives, by_axis(): shard = lax.psum(shard, axis)  206 us
    dot_general x4, matrix products, couple(): jnp.einsum('teij,ktej->kti', blocks, picked, precision=lax.Precision.HIGH...  74.3 us
    dynamic_update_slice x8, other arithmetic, tile_blocks(): lax.map(one_tile, (mine_all, tile_lists, jnp.arange(tile_count, dtype=jnp...  49.1 us
    ppermute x15, starting transfers between devices, padded(): lax.ppermute(head, axis, [((i + 1) % count, i) for i in range(ends)])  47.3 us
    ppermute x15, starting transfers between devices, padded(): lax.ppermute(tail, axis, [(i, (i + 1) % count) for i in range(ends)])  36.1 us
    ppermute x15, waiting for transfers between devices, padded(): lax.ppermute(head, axis, [((i + 1) % count, i) for i in range(ends)])  33.7 us
  transfers between devices with their start and end apart: 30, of which 15 were waited for; matrix products, arithmetic and copies ran while one was open for 1% of the time, Pallas kernels for 0%

commit v1 on v0

v1 whole, which is shorter than its diff:
```python
import functools

import jax
import jax.numpy as jnp
import numpy as np
from jax import lax
from jax.experimental import pallas as pl
from jax.experimental.pallas import tpu as pltpu
from jax.sharding import PartitionSpec as P

ITERS = 4
CUTOFF = 10.0
COULOMB = 0.3
VOLUME = 10.0
TILES = 8
W = 128
F32 = jnp.float32
BF16 = jnp.bfloat16
MIB = 1 << 20
FAR = 1e4
DROP = 1e-9

OFFSETS = np.array([(i % 3 - 1, i // 3 % 3 - 1, i // 9 - 1) for i in range(27)])
HOME = 13
ROWS = 27 * TILES
ENTRIES = 18

VMEM = pl.BlockSpec(memory_space=pltpu.VMEM)
SMEM = pl.BlockSpec(memory_space=pltpu.SMEM)


def surrounded(cells):
    cells = cells[None]
    for axis in ("gx", "gy", "gz"):
        count = lax.axis_size(axis)
        before = lax.ppermute(cells, axis, [(i, (i + 1) % count) for i in range(count)])
        after = lax.ppermute(cells, axis, [((i + 1) % count, i) for i in range(count)])
        cells = jnp.concatenate([before, cells, after], axis=0)
    return cells


def summed(rows):
    for axis in ("gx", "gy", "gz"):
        count = lax.axis_size(axis)
        step = 1
        while step < count:
            rows = rows + lax.ppermute(rows, axis, [(i, i ^ step) for i in range(count)])
            step *= 2
    return rows


def pieces(value):
    high = value.astype(BF16).astype(F32)
    rest = value - high
    middle = rest.astype(BF16).astype(F32)
    return high, middle, rest - middle


def by_kind(kind, table):
    return jnp.where(
        kind < 0.5,
        table[0],
        jnp.where(kind < 1.5, table[1], jnp.where(kind < 2.5, table[2], table[3])),
    )


def build_kernel(edge, lists, far, powers, electro, near, blocks, start, others, others_p, own, floor):
    zero = jnp.zeros((TILES, W), F32)
    one = jnp.ones((TILES, W), F32)

    def atoms(box):
        place = [
            (near[box, 8 * k : 8 * k + 8, :] + (float(OFFSETS[box][k]) - 0.5)) * edge
            for k in range(3)
        ]
        kind = near[box, 24:32, :]
        square = place[0] * place[0] + place[1] * place[1] + place[2] * place[2]
        return place, kind, by_kind(kind, powers), square

    for box in range(27):
        place, kind, power, square = atoms(box)
        rows = []
        for value in place:
            high, middle, low = pieces(value)
            rows += [high, middle, high, middle, low, high]
        rows += [one, one, one] + list(pieces(square + far[box])) + [zero] * 8
        for k, row in enumerate(rows):
            others[k * ROWS + box * 8 : k * ROWS + box * 8 + 8, :] = row
        high, middle, _ = pieces(power)
        for k, row in enumerate([high, middle, high] + [zero] * 5):
            others_p[k * ROWS + box * 8 : k * ROWS + box * 8 + 8, :] = row
        start[16 * box : 16 * box + 8, :] = -by_kind(kind, electro)
        start[16 * box + 8 : 16 * box + 16, :] = -one
    place, kind, power, square = atoms(HOME)
    rows = []
    for value in place:
        high, middle, low = pieces(-2.0 * value)
        rows += [high, high, middle, middle, high, low]
    rows += list(pieces(square)) + [one, one, one]
    high, middle, _ = pieces(power)
    rows += [high, high, middle] + [zero] * (W - 27)
    for k, row in enumerate(rows):
        own[k * 8 : k * 8 + 8, :] = row
    diagonal = lax.broadcasted_iota(jnp.int32, (W, W), 0) == lax.broadcasted_iota(
        jnp.int32, (W, W), 1
    )
    floor[0] = jnp.full((W, W), 1e-12, F32)
    floor[1] = jnp.where(diagonal, 2.0, 1e-12)
    blank = jnp.zeros((24, W), BF16)

    def tile(t, carry):
        left = jnp.transpose(own[pl.ds(t, W, stride=8), :])[:, :32].astype(BF16)

        def entry(e, carry):
            which = lists[t, e]
            right = others[pl.ds(which, 32, stride=ROWS), :].astype(BF16)
            right_p = others_p[pl.ds(which, 8, stride=ROWS), :].astype(BF16)
            right = jnp.concatenate([right, jnp.concatenate([blank, right_p], axis=0)], axis=1)
            both = lax.dot_general(
                left, right, (((1,), (0,)), ((), ())), preferred_element_type=F32
            )
            least = floor[jnp.where(which == HOME * TILES + t, 1, 0)]
            square = jnp.minimum(jnp.maximum(both[:, :W], least), 1.0)
            length = square * lax.rsqrt(square)
            cube = length * square + both[:, W:]
            shield = jnp.exp2(jnp.log2(cube) * (-1.0 / 3.0))
            gap = 1.0 - length
            gap = gap * gap
            shape = (length + 0.5) * (square + 0.2) - 0.05
            blocks[t, e] = (gap * gap) * (shape * shield)
            return carry

        return lax.fori_loop(0, lists.shape[1], entry, carry, unroll=4)

    lax.fori_loop(0, TILES, tile, 0)


def build(lists, far, powers, electro, near, edge):
    entries = lists.shape[1]
    return pl.pallas_call(
        functools.partial(build_kernel, edge),
        out_shape=(
            pltpu.VMEM((TILES, entries, W, W), F32),
            jax.ShapeDtypeStruct((27 * 16, W), F32),
        ),
        in_specs=[SMEM, SMEM, SMEM, SMEM, VMEM],
        out_specs=(VMEM, VMEM),
        scratch_shapes=[
            pltpu.VMEM((32 * ROWS, W), F32),
            pltpu.VMEM((8 * ROWS, W), F32),
            pltpu.VMEM((8 * W, W), F32),
            pltpu.VMEM((2, W, W), F32),
        ],
        compiler_params=pltpu.CompilerParams(vmem_limit_bytes=8 * MIB),
        name="build",
    )(lists, far, powers, electro, near)


def product_kernel(last, lists, scalars, around, kinds, blocks, *rest):
    earlier, (out, total) = rest[:-2], rest[-2:]

    def tile(t, carry):
        def entry(e, sums):
            which = lists[t, e]
            row = which // TILES * 16 + which % TILES
            block = blocks[t, e]
            return (
                sums[0] + block * around[pl.ds(row, 1), :],
                sums[1] + block * around[pl.ds(row + 8, 1), :],
            )

        zero = jnp.zeros((W, W), F32)
        sums = lax.fori_loop(0, lists.shape[1], entry, (zero, zero), unroll=2)
        for k in range(2):
            total[pl.ds(t + 8 * k, 1), :] = jnp.sum(jnp.transpose(sums[k]), axis=0, keepdims=True)
        return carry

    lax.fori_loop(0, TILES, tile, 0)
    kind = kinds[...]
    eta = by_kind(kind, [scalars[2 + k] for k in range(4)])
    home = around[16 * HOME : 16 * HOME + 16, :]
    following = total[...] * scalars[0] + jnp.concatenate([eta, eta], axis=0) * home
    if not last:
        out[...] = following
        return
    basis = [ref[...] for ref in earlier] + [home, following]
    for k in range(2):
        parts = [v[8 * k : 8 * k + 8] for v in basis]
        rows = [parts[i] * parts[j] for i in range(ITERS) for j in range(i, ITERS + 1)] + parts[:ITERS]
        for index, row in enumerate(rows):
            out[2 * index + k : 2 * index + k + 1, :] = jnp.sum(row, axis=0, keepdims=True)
    out[36:40, :] = jnp.zeros((4, W), F32)


def product(lists, scalars, around, kinds, blocks, earlier=()):
    last = bool(earlier)
    return pl.pallas_call(
        functools.partial(product_kernel, last),
        out_shape=jax.ShapeDtypeStruct((40 if last else 16, W), F32),
        in_specs=[SMEM, SMEM, VMEM, VMEM, VMEM] + [VMEM] * len(earlier),
        out_specs=VMEM,
        scratch_shapes=[pltpu.VMEM((16, W), F32)],
        compiler_params=pltpu.CompilerParams(vmem_limit_bytes=8 * MIB),
        name="product",
    )(lists, scalars, around, kinds, blocks, *earlier)


def two_sum(a, b):
    s = a + b
    t = s - a
    return s, (a - (s - t)) + (b - t)


def halves(a):
    t = a * 4097.0
    high = t - (t - a)
    return high, a - high


def add(a, b):
    s, e = two_sum(a[0], b[0])
    return two_sum(s, e + (a[1] + b[1]))


def mul(a, b):
    p = a[0] * b[0]
    ah, al = halves(a[0])
    bh, bl = halves(b[0])
    e = ((ah * bh - p) + ah * bl + al * bh) + al * bl
    return two_sum(p, e + (a[0] * b[1] + a[1] * b[0]))


def neg(a):
    return -a[0], -a[1]


def inverse(a):
    y = 1.0 / a[0]
    guess = (y, jnp.zeros_like(y))
    slip = add((jnp.ones_like(y), jnp.zeros_like(y)), neg(mul(a, guess)))
    return add(guess, mul(guess, slip))


def finish_kernel(scalars, gram, v0, v1, v2, v3, charges, solutions):
    pair = (gram[...], jnp.zeros((40, W), F32))
    shift = W // 2
    while shift:
        pair = add(pair, (pltpu.roll(pair[0], shift, 1), pltpu.roll(pair[1], shift, 1)))
        shift //= 2

    def value(index):
        return pair[0][2 * index : 2 * index + 2], pair[1][2 * index : 2 * index + 2]

    index_of = {}
    for i in range(ITERS):
        for j in range(i, ITERS + 1):
            index_of[i, j] = len(index_of)
    dots = {key: value(index) for key, index in index_of.items()}
    sums = [value(len(index_of) + i) for i in range(ITERS)]

    def dot(i, j):
        return dots[min(i, j), max(i, j)]

    none = jnp.zeros((2, W), F32)
    spread = (jnp.full((2, W), scalars[6], F32), none)
    centre = (jnp.full((2, W), scalars[7], F32), none)
    matrix = {
        (i, j): add(mul(spread, dot(i, j + 1)), mul(centre, dot(i, j)))
        for i in range(ITERS)
        for j in range(i + 1)
    }
    size = [abs(matrix[i, i][0]) for i in range(ITERS)]
    right = [dot(i, 0) for i in range(ITERS)]
    inverses, factors = [], {}
    for k in range(ITERS):
        pivot = matrix[k, k]
        usable = abs(pivot[0]) > DROP * size[k]
        turned = inverse((jnp.where(usable, pivot[0], 1.0), jnp.where(usable, pivot[1], 0.0)))
        turned = (jnp.where(usable, turned[0], 0.0), jnp.where(usable, turned[1], 0.0))
        inverses.append(turned)
        for i in range(k + 1, ITERS):
            factors[i, k] = mul(matrix[i, k], turned)
        for i in range(k + 1, ITERS):
            for j in range(k + 1, i + 1):
                matrix[i, j] = add(matrix[i, j], neg(mul(factors[i, k], matrix[j, k])))
            right[i] = add(right[i], neg(mul(factors[i, k], right[k])))
    weights = [None] * ITERS
    for k in reversed(range(ITERS)):
        weight = mul(right[k], inverses[k])
        for i in range(k + 1, ITERS):
            weight = add(weight, neg(mul(factors[i, k], weights[i])))
        weights[k] = weight
    whole = mul(weights[0], sums[0])
    for k in range(1, ITERS):
        whole = add(whole, mul(weights[k], sums[k]))
    basis = [ref[...] for ref in (v0, v1, v2, v3)]
    parts = []
    for k in range(2):
        part = weights[0][0][k : k + 1] * basis[0][8 * k : 8 * k + 8]
        for i in range(1, ITERS):
            part = part + weights[i][0][k : k + 1] * basis[i][8 * k : 8 * k + 8]
        parts.append(part)
        solutions[8 * k : 8 * k + 8, :] = part
    level = whole[0][0:1] / whole[0][1:2]
    charges[...] = parts[0] - level * parts[1]


def finish(scalars, gram, basis):
    return pl.pallas_call(
        finish_kernel,
        out_shape=(jax.ShapeDtypeStruct((TILES, W), F32), jax.ShapeDtypeStruct((16, W), F32)),
        in_specs=[SMEM] + [VMEM] * 5,
        out_specs=(VMEM, VMEM),
        compiler_params=pltpu.CompilerParams(vmem_limit_bytes=8 * MIB),
        name="finish",
    )(scalars, gram, *basis)


def on_device(positions, types, tile_lists, hardness, electroneg, gamma_table):
    atoms = positions.shape[4]
    edge = (atoms * VOLUME) ** (1.0 / 3.0) / CUTOFF
    box = tile_lists // TILES
    place = (box % 3) * 9 + box // 3 % 3 * 3 + box // 9
    lists = place * TILES + tile_lists % TILES
    inside = jnp.ones((27,), bool)
    for k, axis in enumerate(("gx", "gy", "gz")):
        there = lax.axis_index(axis) + OFFSETS[:, k].astype(np.int32)
        inside = inside & (there >= 0) & (there < lax.axis_size(axis))
    far = jnp.where(inside, 0.0, FAR).astype(F32)
    powers = gamma_table**-1.5 * CUTOFF**-1.5
    least, most = jnp.min(hardness), jnp.max(hardness)
    centre = 0.5 * (least + most) + 1.0
    spread = 0.5 * (most - least) + 1.5
    scale = 20.0 * COULOMB / CUTOFF
    scalars = jnp.concatenate(
        [
            jnp.stack([scale / spread, 1.0 / spread]),
            (hardness - centre) / spread,
            jnp.stack([spread, centre]),
        ]
    )
    kinds = types.reshape(TILES, W).astype(F32)
    cells = jnp.concatenate([positions.reshape(3 * TILES, W), kinds], axis=0)
    near = surrounded(cells)
    blocks, start = build(lists, far, powers, electroneg, near, edge)
    basis = [start[16 * HOME : 16 * HOME + 16]]
    around = start
    for _ in range(ITERS - 1):
        basis.append(product(lists, scalars, around, kinds, blocks))
        around = surrounded(basis[-1]).reshape(27 * 16, W)
    gram = summed(product(lists, scalars, around, kinds, blocks, tuple(basis[:-1])))
    charges, solutions = finish(scalars, gram, basis)
    return charges.reshape(1, 1, 1, atoms), solutions.reshape(1, 1, 1, 2, atoms)


def solution(mesh):
    across = ("gx", "gy", "gz")
    return jax.shard_map(
        on_device,
        mesh=mesh,
        in_specs=(P(*across, None, None), P(*across, None), P(), P(), P(), P()),
        out_specs=(P(*across, None), P(*across, None, None)),
        check_vma=False,
    )
```

time: 524 us -> 173 us (0.33)
  blocking collectives: 206 us -> 0 us
  matrix products: 77.7 us -> 0 us
  other arithmetic: 79.2 us -> 6.87 us
  Pallas kernels: 0 us -> 54.3 us
  starting transfers between devices: 83.4 us -> 53.4 us
  local copies, waits for them, and re-layouts: 22.4 us -> 1.53 us
  waiting for transfers between devices: 40.1 us -> 50.2 us
  loops' own time: 5.87 us -> 0 us
    psum x25 -> x0, blocking collectives: 206 us -> none  [by_axis(): shard = lax.psum(shard, axis)]
    dot_general x7 -> x0, matrix products: 77.7 us -> none  [the longest x4 74.3 us: couple(): jnp.einsum('teij,ktej->kti', blocks, picked, precision=lax.Precision.HIGH...]
    pallas_call x0 -> x6, Pallas kernels: none -> 54.3 us  [the longest x4 27.6 us: product(): pl.pallas_call(functools.partial(product_kernel, last), out_shape=jax.Sha...]
    dynamic_update_slice x8 -> x0, other arithmetic: 49.1 us -> none  [tile_blocks(): lax.map(one_tile, (mine_all, tile_lists, jnp.arange(tile_count, dtype=jnp...]
    ppermute x30 -> x32, starting transfers between devices: 83.4 us -> 53.4 us  [the longest x12 32 us: surrounded(): lax.ppermute(cells, axis, [((i + 1) % count, i) for i in range(count)])]
    gather x12 -> x0, local copies, waits for them, and re-layouts: 13.3 us -> none  [the longest x4 8.54 us: couple(): picked = nearby_vectors[:, tile_lists]]
    ppermute x30 -> x32, waiting for transfers between devices: 40.1 us -> 50.2 us  [the longest x8 23.1 us: summed(): lax.ppermute(rows, axis, [(i, i ^ step) for i in range(count)])]
    reduce_sum x10 -> x0, other arithmetic: 9.54 us -> none  [the longest x8 9.13 us: one_tile(): spacing = jnp.sqrt(jnp.sum(separation * separation, axis=0))]
  transfers between devices with their start and end apart: 30 -> 32, of which waited for: 15 -> 24; matrix products, arithmetic and copies ran while one was open for 1% -> 3% of each run, Pallas kernels for 0% -> 0%
where the time goes in v1:
time: 173 us; the launch traced here: 170 us
  Pallas kernels  54.3 us (31%)
  starting transfers between devices  53.4 us (31%)
  waiting for transfers between devices  50.2 us (29%)
  other arithmetic  6.87 us (4%)
  between operations  3.67 us (2%)
    ppermute x12, starting transfers between devices, surrounded(): lax.ppermute(cells, axis, [((i + 1) % count, i) for i in range(count)])  32 us
    pallas_call x4, Pallas kernels, product(): pl.pallas_call(functools.partial(product_kernel, last), out_shape=jax.Sha...  27.6 us
    pallas_call x1, Pallas kernels, build(): pl.pallas_call(functools.partial(build_kernel, edge), out_shape=(pltpu.VM...  24.3 us
    ppermute x8, waiting for transfers between devices, summed(): lax.ppermute(rows, axis, [(i, i ^ step) for i in range(count)])  23.1 us
    ppermute x12, waiting for transfers between devices, surrounded(): lax.ppermute(cells, axis, [(i, (i + 1) % count) for i in range(count)])  22.6 us
    ppermute x8, starting transfers between devices, summed(): lax.ppermute(rows, axis, [(i, i ^ step) for i in range(count)])  12.4 us
    ppermute x12, starting transfers between devices, surrounded(): lax.ppermute(cells, axis, [(i, (i + 1) % count) for i in range(count)])  9.02 us
    ppermute x12, waiting for transfers between devices, surrounded(): lax.ppermute(cells, axis, [((i + 1) % count, i) for i in range(count)])  4.44 us
  transfers between devices with their start and end apart: 32, of which 24 were waited for; matrix products, arithmetic and copies ran while one was open for 3% of the time, Pallas kernels for 0%

profile of v1, /device:TPU:16, one launch (start us, length us, event | category | flops | bytes accessed | tf_op | source)
XLA Modules:
  0.0 170.0 jit_solution(6603024806278776895)
XLA Ops:
  10.5 4.2 %collective-permute-start.3 = (f32[3,32,128]{2,1,0:T(8,128)S(1)}, f32[3,32,128]{2,1,0:T(8,128)S(1)}, u32[]{:S(2)}, u32[]{:S(2)}) collective-permute-start(f32[3,32,128]{2,1,0:T(8,128)S(1)} %pad_maximum_fusion), channel_id=1, source_target_pairs={{8,0},{16,8},{24,16},{32,24},{40,32},{48,40},{56,48},{0,56},{9,1},... | collective-permute-start | bytes 147464 | tf_op jit(solution)/shard_map/ppermute | solution.py:37
  17.0 2.0 %collective-permute-start.4 = (f32[9,32,128]{2,1,0:T(8,128)S(1)}, f32[9,32,128]{2,1,0:T(8,128)S(1)}, u32[]{:S(2)}, u32[]{:S(2)}) collective-permute-start(f32[9,32,128]{2,1,0:T(8,128)S(1)} %constant_dynamic-update-slice_fusion), channel_id=1, source_target_pairs={{0,1},{1,2},{2,3},{3,4},{4,5},{5,6},{6,7},{7,0},{8,9},{9,10},{10,1... | collective-permute-start | bytes 442376 | tf_op jit(solution)/shard_map/ppermute | solution.py:36
  19.7 4.0 %collective-permute-start.5 = (f32[9,32,128]{2,1,0:T(8,128)S(1)}, f32[9,32,128]{2,1,0:T(8,128)S(1)}, u32[]{:S(2)}, u32[]{:S(2)}) collective-permute-start(f32[9,32,128]{2,1,0:T(8,128)S(1)} %constant_dynamic-update-slice_fusion), channel_id=1, source_target_pairs={{1,0},{2,1},{3,2},{4,3},{5,4},{6,5},{7,6},{0,7},{9,8},{10,9},{11,1... | collective-permute-start | bytes 442376 | tf_op jit(solution)/shard_map/ppermute | solution.py:37
  23.6 3.3 %collective-permute-done.4 = f32[9,32,128]{2,1,0:T(8,128)S(1)} collective-permute-done((f32[9,32,128]{2,1,0:T(8,128)S(1)}, f32[9,32,128]{2,1,0:T(8,128)S(1)}, u32[]{:S(2)}, u32[]{:S(2)}) %collective-permute-start.4) | collective-permute-done | bytes 147488 | tf_op jit(solution)/shard_map/ppermute | solution.py:36
  28.4 24.3 %build.1 = (f32[8,36,128,128]{3,2,1,0:T(8,128)S(1)}, f32[432,128]{1,0:T(8,128)S(1)}) custom-call(s32[8,36]{1,0:T(8,128)S(1)} %fusion.4.lists, f32[27]{0:T(128)S(1)} %and_select_fusion.far, f32[4]{0:T(128)S(1)} %power_multiply_fusion.powers, f32[4]{0:T(128)S(1)} %copy-done, f32[27,32,128]{2,1,0:T(8,128)S(1)} %constant_dynamic-update-slice_fusion.5.near), custom_call_target="tpu_custom_call" | custom-call | tf_op jit(solution)/shard_map/build/pallas_call | solution.py:140
  52.7 6.9 %product.4.rest_1_.v1 = f32[16,128]{1,0:T(8,128)S(1)} custom-call(s32[8,36]{1,0:T(8,128)S(1)} %fusion.4.lists, f32[8]{0:T(128)S(1)} %concatenate.50.scalars, f32[432,128]{1,0:T(8,128)S(1)} %get-tuple-element.6.around, f32[8,128]{1,0:T(8,128)S(1)} %bitcast.37, f32[8,36,128,128]{3,2,1,0:T(8,128)S(1)} %get-tuple-element.7.blocks), custom_call_target="tpu_custom_call" | custom-call | tf_op jit(solution)/shard_map/product/pallas_call | solution.py:197
  63.1 5.6 %collective-permute-start.9 = (f32[3,16,128]{2,1,0:T(8,128)S(1)}, f32[3,16,128]{2,1,0:T(8,128)S(1)}, u32[]{:S(2)}, u32[]{:S(2)}) collective-permute-start(f32[3,16,128]{2,1,0:T(8,128)S(1)} %pad_maximum_fusion.1), channel_id=1, source_target_pairs={{8,0},{16,8},{24,16},{32,24},{40,32},{48,40},{56,48},{0,56},{9,1},... | collective-permute-start | bytes 73736 | tf_op jit(solution)/shard_map/ppermute | solution.py:37
  68.8 1.8 %collective-permute-done.8 = f32[3,16,128]{2,1,0:T(8,128)S(1)} collective-permute-done((f32[3,16,128]{2,1,0:T(8,128)S(1)}, f32[3,16,128]{2,1,0:T(8,128)S(1)}, u32[]{:S(2)}, u32[]{:S(2)}) %collective-permute-start.8) | collective-permute-done | bytes 24608 | tf_op jit(solution)/shard_map/ppermute | solution.py:36
  70.7 3.2 %collective-permute-start.11 = (f32[9,16,128]{2,1,0:T(8,128)S(1)}, f32[9,16,128]{2,1,0:T(8,128)S(1)}, u32[]{:S(2)}, u32[]{:S(2)}) collective-permute-start(f32[9,16,128]{2,1,0:T(8,128)S(1)} %constant_dynamic-update-slice_fusion.12), channel_id=1, source_target_pairs={{1,0},{2,1},{3,2},{4,3},{5,4},{6,5},{7,6},{0,7},{9,8},{10,9},{11,1... | collective-permute-start | bytes 221192 | tf_op jit(solution)/shard_map/ppermute | solution.py:37
  73.9 2.3 %collective-permute-done.10 = f32[9,16,128]{2,1,0:T(8,128)S(1)} collective-permute-done((f32[9,16,128]{2,1,0:T(8,128)S(1)}, f32[9,16,128]{2,1,0:T(8,128)S(1)}, u32[]{:S(2)}, u32[]{:S(2)}) %collective-permute-start.10) | collective-permute-done | bytes 73760 | tf_op jit(solution)/shard_map/ppermute | solution.py:36
  76.3 6.9 %product.5.rest_2_.v2 = f32[16,128]{1,0:T(8,128)S(1)} custom-call(s32[8,36]{1,0:T(8,128)S(1)} %fusion.4.lists, f32[8]{0:T(128)S(1)} %concatenate.50.scalars, f32[432,128]{1,0:T(8,128)S(1)} %bitcast.25, f32[8,128]{1,0:T(8,128)S(1)} %bitcast.38, f32[8,36,128,128]{3,2,1,0:T(8,128)S(1)} %get-tuple-element.7.blocks), custom_call_target="tpu_custom_call" | custom-call | tf_op jit(solution)/shard_map/product/pallas_call | solution.py:197
  86.5 5.6 %collective-permute-start.15 = (f32[3,16,128]{2,1,0:T(8,128)S(1)}, f32[3,16,128]{2,1,0:T(8,128)S(1)}, u32[]{:S(2)}, u32[]{:S(2)}) collective-permute-start(f32[3,16,128]{2,1,0:T(8,128)S(1)} %pad_maximum_fusion.2), channel_id=1, source_target_pairs={{8,0},{16,8},{24,16},{32,24},{40,32},{48,40},{56,48},{0,56},{9,1},... | collective-permute-start | bytes 73736 | tf_op jit(solution)/shard_map/ppermute | solution.py:37
  92.1 1.8 %collective-permute-done.14 = f32[3,16,128]{2,1,0:T(8,128)S(1)} collective-permute-done((f32[3,16,128]{2,1,0:T(8,128)S(1)}, f32[3,16,128]{2,1,0:T(8,128)S(1)}, u32[]{:S(2)}, u32[]{:S(2)}) %collective-permute-start.14) | collective-permute-done | bytes 24608 | tf_op jit(solution)/shard_map/ppermute | solution.py:36
  94.0 2.1 %collective-permute-start.16 = (f32[9,16,128]{2,1,0:T(8,128)S(1)}, f32[9,16,128]{2,1,0:T(8,128)S(1)}, u32[]{:S(2)}, u32[]{:S(2)}) collective-permute-start(f32[9,16,128]{2,1,0:T(8,128)S(1)} %constant_dynamic-update-slice_fusion.24), channel_id=1, source_target_pairs={{0,1},{1,2},{2,3},{3,4},{4,5},{5,6},{6,7},{7,0},{8,9},{9,10},{10,1... | collective-permute-start | bytes 221192 | tf_op jit(solution)/shard_map/ppermute | solution.py:36
  97.3 2.3 %collective-permute-done.16 = f32[9,16,128]{2,1,0:T(8,128)S(1)} collective-permute-done((f32[9,16,128]{2,1,0:T(8,128)S(1)}, f32[9,16,128]{2,1,0:T(8,128)S(1)}, u32[]{:S(2)}, u32[]{:S(2)}) %collective-permute-start.16) | collective-permute-done | bytes 73760 | tf_op jit(solution)/shard_map/ppermute | solution.py:36
  100.4 6.9 %product.6.v3 = f32[16,128]{1,0:T(8,128)S(1)} custom-call(s32[8,36]{1,0:T(8,128)S(1)} %fusion.4.lists, f32[8]{0:T(128)S(1)} %concatenate.50.scalars, f32[432,128]{1,0:T(8,128)S(1)} %bitcast.26, f32[8,128]{1,0:T(8,128)S(1)} %bitcast.39, f32[8,36,128,128]{3,2,1,0:T(8,128)S(1)} %get-tuple-element.7.blocks), custom_call_target="tpu_custom_call" | custom-call | tf_op jit(solution)/shard_map/product/pallas_call | solution.py:197
  110.5 5.6 %collective-permute-start.21 = (f32[3,16,128]{2,1,0:T(8,128)S(1)}, f32[3,16,128]{2,1,0:T(8,128)S(1)}, u32[]{:S(2)}, u32[]{:S(2)}) collective-permute-start(f32[3,16,128]{2,1,0:T(8,128)S(1)} %pad_maximum_fusion.3), channel_id=1, source_target_pairs={{8,0},{16,8},{24,16},{32,24},{40,32},{48,40},{56,48},{0,56},{9,1},... | collective-permute-start | bytes 73736 | tf_op jit(solution)/shard_map/ppermute | solution.py:37
  118.0 2.1 %collective-permute-start.22 = (f32[9,16,128]{2,1,0:T(8,128)S(1)}, f32[9,16,128]{2,1,0:T(8,128)S(1)}, u32[]{:S(2)}, u32[]{:S(2)}) collective-permute-start(f32[9,16,128]{2,1,0:T(8,128)S(1)} %constant_dynamic-update-slice_fusion.36), channel_id=1, source_target_pairs={{0,1},{1,2},{2,3},{3,4},{4,5},{5,6},{6,7},{7,0},{8,9},{9,10},{10,1... | collective-permute-start | bytes 221192 | tf_op jit(solution)/shard_map/ppermute | solution.py:36
  121.3 2.3 %collective-permute-done.22 = f32[9,16,128]{2,1,0:T(8,128)S(1)} collective-permute-done((f32[9,16,128]{2,1,0:T(8,128)S(1)}, f32[9,16,128]{2,1,0:T(8,128)S(1)}, u32[]{:S(2)}, u32[]{:S(2)}) %collective-permute-start.22) | collective-permute-done | bytes 73760 | tf_op jit(solution)/shard_map/ppermute | solution.py:36
  124.5 6.9 %product.7 = f32[40,128]{1,0:T(8,128)S(1)} custom-call(s32[8,36]{1,0:T(8,128)S(1)} %fusion.4.lists, f32[8]{0:T(128)S(1)} %concatenate.50.scalars, f32[432,128]{1,0:T(8,128)S(1)} %bitcast.27, f32[8,128]{1,0:T(8,128)S(1)} %bitcast.40, f32[8,36,128,128]{3,2,1,0:T(8,128)S(1)} %get-tuple-element.7.blocks, f32[16,128]{1,0:T(8,128)S(1)} %slice.3.rest_0_.v0, ...), custom_call_target="tpu_custom_call" | custom-call | tf_op jit(solution)/shard_map/product/pallas_call | solution.py:197
  133.9 2.6 %collective-permute-done.25 = f32[40,128]{1,0:T(8,128)S(1)} collective-permute-done((f32[40,128]{1,0:T(8,128)S(1)}, f32[40,128]{1,0:T(8,128)S(1)}, u32[]{:S(2)}, u32[]{:S(2)}) %collective-permute-start.25) | collective-permute-done | bytes 20512 | tf_op jit(solution)/shard_map/ppermute | solution.py:47
  136.5 3.8 %collective-permute-done.26 = f32[40,128]{1,0:T(8,128)S(1)} collective-permute-done((f32[40,128]{1,0:T(8,128)S(1)}, f32[40,128]{1,0:T(8,128)S(1)}, u32[]{:S(2)}, u32[]{:S(2)}) %collective-permute-start.26) | collective-permute-done | bytes 20512 | tf_op jit(solution)/shard_map/ppermute | solution.py:47
  140.3 2.6 %collective-permute-start.27 = (f32[40,128]{1,0:T(8,128)S(1)}, f32[40,128]{1,0:T(8,128)S(1)}, u32[]{:S(2)}, u32[]{:S(2)}) collective-permute-start(f32[40,128]{1,0:T(8,128)S(1)} %add.94), channel_id=1, source_target_pairs={{0,16},{8,24},{16,0},{24,8},{32,48},{40,56},{48,32},{56,40},{1,17}... | collective-permute-start | bytes 61448 | tf_op jit(solution)/shard_map/ppermute | solution.py:47
  142.9 2.7 %collective-permute-done.27 = f32[40,128]{1,0:T(8,128)S(1)} collective-permute-done((f32[40,128]{1,0:T(8,128)S(1)}, f32[40,128]{1,0:T(8,128)S(1)}, u32[]{:S(2)}, u32[]{:S(2)}) %collective-permute-start.27) | collective-permute-done | bytes 20512 | tf_op jit(solution)/shard_map/ppermute | solution.py:47
  145.6 2.0 %collective-permute-start.28 = (f32[40,128]{1,0:T(8,128)S(1)}, f32[40,128]{1,0:T(8,128)S(1)}, u32[]{:S(2)}, u32[]{:S(2)}) collective-permute-start(f32[40,128]{1,0:T(8,128)S(1)} %add.95), channel_id=1, source_target_pairs={{0,32},{8,40},{16,48},{24,56},{32,0},{40,8},{48,16},{56,24},{1,33}... | collective-permute-start | bytes 61448 | tf_op jit(solution)/shard_map/ppermute | solution.py:47
  147.6 3.3 %collective-permute-done.28 = f32[40,128]{1,0:T(8,128)S(1)} collective-permute-done((f32[40,128]{1,0:T(8,128)S(1)}, f32[40,128]{1,0:T(8,128)S(1)}, u32[]{:S(2)}, u32[]{:S(2)}) %collective-permute-start.28) | collective-permute-done | bytes 20512 | tf_op jit(solution)/shard_map/ppermute | solution.py:47
  152.5 2.2 %collective-permute-done.29 = f32[40,128]{1,0:T(8,128)S(1)} collective-permute-done((f32[40,128]{1,0:T(8,128)S(1)}, f32[40,128]{1,0:T(8,128)S(1)}, u32[]{:S(2)}, u32[]{:S(2)}) %collective-permute-start.29) | collective-permute-done | bytes 20512 | tf_op jit(solution)/shard_map/ppermute | solution.py:47
  154.6 2.3 %collective-permute-start.30 = (f32[40,128]{1,0:T(8,128)S(1)}, f32[40,128]{1,0:T(8,128)S(1)}, u32[]{:S(2)}, u32[]{:S(2)}) collective-permute-start(f32[40,128]{1,0:T(8,128)S(1)} %add.97), channel_id=1, source_target_pairs={{0,2},{1,3},{2,0},{3,1},{4,6},{5,7},{6,4},{7,5},{8,10},{9,11},{10,... | collective-permute-start | bytes 61448 | tf_op jit(solution)/shard_map/ppermute | solution.py:47
  157.0 2.3 %collective-permute-done.30 = f32[40,128]{1,0:T(8,128)S(1)} collective-permute-done((f32[40,128]{1,0:T(8,128)S(1)}, f32[40,128]{1,0:T(8,128)S(1)}, u32[]{:S(2)}, u32[]{:S(2)}) %collective-permute-start.30) | collective-permute-done | bytes 20512 | tf_op jit(solution)/shard_map/ppermute | solution.py:47
  159.3 2.6 %collective-permute-start.31 = (f32[40,128]{1,0:T(8,128)S(1)}, f32[40,128]{1,0:T(8,128)S(1)}, u32[]{:S(2)}, u32[]{:S(2)}) collective-permute-start(f32[40,128]{1,0:T(8,128)S(1)} %add.98), channel_id=1, source_target_pairs={{0,4},{1,5},{2,6},{3,7},{4,0},{5,1},{6,2},{7,3},{8,12},{9,13},{10,... | collective-permute-start | bytes 61448 | tf_op jit(solution)/shard_map/ppermute | solution.py:47
  161.9 5.1 %collective-permute-done.31 = f32[40,128]{1,0:T(8,128)S(1)} collective-permute-done((f32[40,128]{1,0:T(8,128)S(1)}, f32[40,128]{1,0:T(8,128)S(1)}, u32[]{:S(2)}, u32[]{:S(2)}) %collective-permute-start.31) | collective-permute-done | bytes 20512 | tf_op jit(solution)/shard_map/ppermute | solution.py:47
  167.0 2.4 %finish.1 = (f32[8,128]{1,0:T(8,128)}, f32[16,128]{1,0:T(8,128)S(1)}) custom-call(f32[8]{0:T(128)S(1)} %concatenate.50.scalars, f32[40,128]{1,0:T(8,128)S(1)} %add.99.gram, f32[16,128]{1,0:T(8,128)S(1)} %slice.3.rest_0_.v0, f32[16,128]{1,0:T(8,128)S(1)} %product.4.rest_1_.v1, f32[16,128]{1,0:T(8,128)S(1)} %product.5.rest_2_.v2, f32[16,128]{1,0:T(8,128)S(1)} %product.6.v3), custom_call_target="tpu_custom_call" | custom-call | tf_op jit(solution)/shard_map/finish/pallas_call | solution.py:309
  (110 shorter events, 32.2 us)
Async XLA Ops:
  2.0 6.0 %collective-permute-start.1 = (f32[1,32,128]{2,1,0:T(8,128)S(1)}, f32[1,32,128]{2,1,0:T(8,128)S(1)}, u32[]{:S(2)}, u32[]{:S(2)}) collective-permute-start(f32[1,32,128]{2,1,0:T(8,128)S(1)} %maximum_bitcast_fusion), channel_id=1, source_target_pairs={{64,0},{128,64},{192,128},{0,192},{65,1},{129,65},{193,129},{1,193... | collective-permute-start | bytes 49160 | tf_op jit(solution)/shard_map/ppermute | solution.py:37
  2.8 5.3 %collective-permute-start = (f32[1,32,128]{2,1,0:T(8,128)S(1)}, f32[1,32,128]{2,1,0:T(8,128)S(1)}, u32[]{:S(2)}, u32[]{:S(2)}) collective-permute-start(f32[1,32,128]{2,1,0:T(8,128)S(1)} %maximum_bitcast_fusion), channel_id=1, source_target_pairs={{0,64},{64,128},{128,192},{192,0},{1,65},{65,129},{129,193},{193,1... | collective-permute-start | bytes 49160 | tf_op jit(solution)/shard_map/ppermute | solution.py:36
  8.1 8.2 %collective-permute-start.2 = (f32[3,32,128]{2,1,0:T(8,128)S(1)}, f32[3,32,128]{2,1,0:T(8,128)S(1)}, u32[]{:S(2)}, u32[]{:S(2)}) collective-permute-start(f32[3,32,128]{2,1,0:T(8,128)S(1)} %pad_maximum_fusion), channel_id=1, source_target_pairs={{0,8},{8,16},{16,24},{24,32},{32,40},{40,48},{48,56},{56,0},{1,9},... | collective-permute-start | bytes 147464 | tf_op jit(solution)/shard_map/ppermute | solution.py:36
  10.5 6.5 %collective-permute-start.3 = (f32[3,32,128]{2,1,0:T(8,128)S(1)}, f32[3,32,128]{2,1,0:T(8,128)S(1)}, u32[]{:S(2)}, u32[]{:S(2)}) collective-permute-start(f32[3,32,128]{2,1,0:T(8,128)S(1)} %pad_maximum_fusion), channel_id=1, source_target_pairs={{8,0},{16,8},{24,16},{32,24},{40,32},{48,40},{56,48},{0,56},{9,1},... | collective-permute-start | bytes 147464 | tf_op jit(solution)/shard_map/ppermute | solution.py:37
  17.0 9.9 %collective-permute-start.4 = (f32[9,32,128]{2,1,0:T(8,128)S(1)}, f32[9,32,128]{2,1,0:T(8,128)S(1)}, u32[]{:S(2)}, u32[]{:S(2)}) collective-permute-start(f32[9,32,128]{2,1,0:T(8,128)S(1)} %constant_dynamic-update-slice_fusion), channel_id=1, source_target_pairs={{0,1},{1,2},{2,3},{3,4},{4,5},{5,6},{6,7},{7,0},{8,9},{9,10},{10,1... | collective-permute-start | bytes 442376 | tf_op jit(solution)/shard_map/ppermute | solution.py:36
  19.7 8.1 %collective-permute-start.5 = (f32[9,32,128]{2,1,0:T(8,128)S(1)}, f32[9,32,128]{2,1,0:T(8,128)S(1)}, u32[]{:S(2)}, u32[]{:S(2)}) collective-permute-start(f32[9,32,128]{2,1,0:T(8,128)S(1)} %constant_dynamic-update-slice_fusion), channel_id=1, source_target_pairs={{1,0},{2,1},{3,2},{4,3},{5,4},{6,5},{7,6},{0,7},{9,8},{10,9},{11,1... | collective-permute-start | bytes 442376 | tf_op jit(solution)/shard_map/ppermute | solution.py:37
  59.6 1.8 %collective-permute-start.7 = (f32[1,16,128]{2,1,0:T(8,128)S(1)}, f32[1,16,128]{2,1,0:T(8,128)S(1)}, u32[]{:S(2)}, u32[]{:S(2)}) collective-permute-start(f32[1,16,128]{2,1,0:T(8,128)S(1)} %bitcast.28), channel_id=1, source_target_pairs={{64,0},{128,64},{192,128},{0,192},{65,1},{129,65},{193,129},{1,193... | collective-permute-start | bytes 24584 | tf_op jit(solution)/shard_map/ppermute | solution.py:37
  60.0 3.1 %collective-permute-start.6 = (f32[1,16,128]{2,1,0:T(8,128)S(1)}, f32[1,16,128]{2,1,0:T(8,128)S(1)}, u32[]{:S(2)}, u32[]{:S(2)}) collective-permute-start(f32[1,16,128]{2,1,0:T(8,128)S(1)} %bitcast.29), channel_id=1, source_target_pairs={{0,64},{64,128},{128,192},{192,0},{1,65},{65,129},{129,193},{193,1... | collective-permute-start | bytes 24584 | tf_op jit(solution)/shard_map/ppermute | solution.py:36
  63.1 7.4 %collective-permute-start.8 = (f32[3,16,128]{2,1,0:T(8,128)S(1)}, f32[3,16,128]{2,1,0:T(8,128)S(1)}, u32[]{:S(2)}, u32[]{:S(2)}) collective-permute-start(f32[3,16,128]{2,1,0:T(8,128)S(1)} %pad_maximum_fusion.1), channel_id=1, source_target_pairs={{0,8},{8,16},{16,24},{24,32},{32,40},{40,48},{48,56},{56,0},{1,9},... | collective-permute-start | bytes 73736 | tf_op jit(solution)/shard_map/ppermute | solution.py:36
  63.1 7.5 %collective-permute-start.9 = (f32[3,16,128]{2,1,0:T(8,128)S(1)}, f32[3,16,128]{2,1,0:T(8,128)S(1)}, u32[]{:S(2)}, u32[]{:S(2)}) collective-permute-start(f32[3,16,128]{2,1,0:T(8,128)S(1)} %pad_maximum_fusion.1), channel_id=1, source_target_pairs={{8,0},{16,8},{24,16},{32,24},{40,32},{48,40},{56,48},{0,56},{9,1},... | collective-permute-start | bytes 73736 | tf_op jit(solution)/shard_map/ppermute | solution.py:37
  70.6 5.6 %collective-permute-start.10 = (f32[9,16,128]{2,1,0:T(8,128)S(1)}, f32[9,16,128]{2,1,0:T(8,128)S(1)}, u32[]{:S(2)}, u32[]{:S(2)}) collective-permute-start(f32[9,16,128]{2,1,0:T(8,128)S(1)} %constant_dynamic-update-slice_fusion.12), channel_id=1, source_target_pairs={{0,1},{1,2},{2,3},{3,4},{4,5},{5,6},{6,7},{7,0},{8,9},{9,10},{10,1... | collective-permute-start | bytes 221192 | tf_op jit(solution)/shard_map/ppermute | solution.py:36
  70.7 5.6 %collective-permute-start.11 = (f32[9,16,128]{2,1,0:T(8,128)S(1)}, f32[9,16,128]{2,1,0:T(8,128)S(1)}, u32[]{:S(2)}, u32[]{:S(2)}) collective-permute-start(f32[9,16,128]{2,1,0:T(8,128)S(1)} %constant_dynamic-update-slice_fusion.12), channel_id=1, source_target_pairs={{1,0},{2,1},{3,2},{4,3},{5,4},{6,5},{7,6},{0,7},{9,8},{10,9},{11,1... | collective-permute-start | bytes 221192 | tf_op jit(solution)/shard_map/ppermute | solution.py:37
  83.2 1.5 collective-permute-start.13
  83.3 3.2 %collective-permute-start.12 = (f32[1,16,128]{2,1,0:T(8,128)S(1)}, f32[1,16,128]{2,1,0:T(8,128)S(1)}, u32[]{:S(2)}, u32[]{:S(2)}) collective-permute-start(f32[1,16,128]{2,1,0:T(8,128)S(1)} %bitcast.32), channel_id=1, source_target_pairs={{0,64},{64,128},{128,192},{192,0},{1,65},{65,129},{129,193},{193,1... | collective-permute-start | bytes 24584 | tf_op jit(solution)/shard_map/ppermute | solution.py:36
  86.5 7.4 %collective-permute-start.14 = (f32[3,16,128]{2,1,0:T(8,128)S(1)}, f32[3,16,128]{2,1,0:T(8,128)S(1)}, u32[]{:S(2)}, u32[]{:S(2)}) collective-permute-start(f32[3,16,128]{2,1,0:T(8,128)S(1)} %pad_maximum_fusion.2), channel_id=1, source_target_pairs={{0,8},{8,16},{16,24},{24,32},{32,40},{40,48},{48,56},{56,0},{1,9},... | collective-permute-start | bytes 73736 | tf_op jit(solution)/shard_map/ppermute | solution.py:36
  86.5 7.5 %collective-permute-start.15 = (f32[3,16,128]{2,1,0:T(8,128)S(1)}, f32[3,16,128]{2,1,0:T(8,128)S(1)}, u32[]{:S(2)}, u32[]{:S(2)}) collective-permute-start(f32[3,16,128]{2,1,0:T(8,128)S(1)} %pad_maximum_fusion.2), channel_id=1, source_target_pairs={{8,0},{16,8},{24,16},{32,24},{40,32},{48,40},{56,48},{0,56},{9,1},... | collective-permute-start | bytes 73736 | tf_op jit(solution)/shard_map/ppermute | solution.py:37
  94.0 5.6 %collective-permute-start.16 = (f32[9,16,128]{2,1,0:T(8,128)S(1)}, f32[9,16,128]{2,1,0:T(8,128)S(1)}, u32[]{:S(2)}, u32[]{:S(2)}) collective-permute-start(f32[9,16,128]{2,1,0:T(8,128)S(1)} %constant_dynamic-update-slice_fusion.24), channel_id=1, source_target_pairs={{0,1},{1,2},{2,3},{3,4},{4,5},{5,6},{6,7},{7,0},{8,9},{9,10},{10,1... | collective-permute-start | bytes 221192 | tf_op jit(solution)/shard_map/ppermute | solution.py:36
  96.0 4.4 %collective-permute-start.17 = (f32[9,16,128]{2,1,0:T(8,128)S(1)}, f32[9,16,128]{2,1,0:T(8,128)S(1)}, u32[]{:S(2)}, u32[]{:S(2)}) collective-permute-start(f32[9,16,128]{2,1,0:T(8,128)S(1)} %constant_dynamic-update-slice_fusion.24), channel_id=1, source_target_pairs={{1,0},{2,1},{3,2},{4,3},{5,4},{6,5},{7,6},{0,7},{9,8},{10,9},{11,1... | collective-permute-start | bytes 221192 | tf_op jit(solution)/shard_map/ppermute | solution.py:37
  107.3 1.5 collective-permute-start.19
  107.4 3.2 %collective-permute-start.18 = (f32[1,16,128]{2,1,0:T(8,128)S(1)}, f32[1,16,128]{2,1,0:T(8,128)S(1)}, u32[]{:S(2)}, u32[]{:S(2)}) collective-permute-start(f32[1,16,128]{2,1,0:T(8,128)S(1)} %bitcast.42), channel_id=1, source_target_pairs={{0,64},{64,128},{128,192},{192,0},{1,65},{65,129},{129,193},{193,1... | collective-permute-start | bytes 24584 | tf_op jit(solution)/shard_map/ppermute | solution.py:36
  110.5 7.4 %collective-permute-start.20 = (f32[3,16,128]{2,1,0:T(8,128)S(1)}, f32[3,16,128]{2,1,0:T(8,128)S(1)}, u32[]{:S(2)}, u32[]{:S(2)}) collective-permute-start(f32[3,16,128]{2,1,0:T(8,128)S(1)} %pad_maximum_fusion.3), channel_id=1, source_target_pairs={{0,8},{8,16},{16,24},{24,32},{32,40},{40,48},{48,56},{56,0},{1,9},... | collective-permute-start | bytes 73736 | tf_op jit(solution)/shard_map/ppermute | solution.py:36
  110.5 7.5 %collective-permute-start.21 = (f32[3,16,128]{2,1,0:T(8,128)S(1)}, f32[3,16,128]{2,1,0:T(8,128)S(1)}, u32[]{:S(2)}, u32[]{:S(2)}) collective-permute-start(f32[3,16,128]{2,1,0:T(8,128)S(1)} %pad_maximum_fusion.3), channel_id=1, source_target_pairs={{8,0},{16,8},{24,16},{32,24},{40,32},{48,40},{56,48},{0,56},{9,1},... | collective-permute-start | bytes 73736 | tf_op jit(solution)/shard_map/ppermute | solution.py:37
  118.0 5.6 %collective-permute-start.22 = (f32[9,16,128]{2,1,0:T(8,128)S(1)}, f32[9,16,128]{2,1,0:T(8,128)S(1)}, u32[]{:S(2)}, u32[]{:S(2)}) collective-permute-start(f32[9,16,128]{2,1,0:T(8,128)S(1)} %constant_dynamic-update-slice_fusion.36), channel_id=1, source_target_pairs={{0,1},{1,2},{2,3},{3,4},{4,5},{5,6},{6,7},{7,0},{8,9},{9,10},{10,1... | collective-permute-start | bytes 221192 | tf_op jit(solution)/shard_map/ppermute | solution.py:36
  120.1 4.4 %collective-permute-start.23 = (f32[9,16,128]{2,1,0:T(8,128)S(1)}, f32[9,16,128]{2,1,0:T(8,128)S(1)}, u32[]{:S(2)}, u32[]{:S(2)}) collective-permute-start(f32[9,16,128]{2,1,0:T(8,128)S(1)} %constant_dynamic-update-slice_fusion.36), channel_id=1, source_target_pairs={{1,0},{2,1},{3,2},{4,3},{5,4},{6,5},{7,6},{0,7},{9,8},{10,9},{11,1... | collective-permute-start | bytes 221192 | tf_op jit(solution)/shard_map/ppermute | solution.py:37
  131.4 1.3 collective-permute-start.24
  132.7 3.8 %collective-permute-start.25 = (f32[40,128]{1,0:T(8,128)S(1)}, f32[40,128]{1,0:T(8,128)S(1)}, u32[]{:S(2)}, u32[]{:S(2)}) collective-permute-start(f32[40,128]{1,0:T(8,128)S(1)} %add.92), channel_id=1, source_target_pairs={{0,128},{64,192},{128,0},{192,64},{1,129},{65,193},{129,1},{193,65... | collective-permute-start | bytes 61448 | tf_op jit(solution)/shard_map/ppermute | solution.py:47
  136.5 3.8 %collective-permute-start.26 = (f32[40,128]{1,0:T(8,128)S(1)}, f32[40,128]{1,0:T(8,128)S(1)}, u32[]{:S(2)}, u32[]{:S(2)}) collective-permute-start(f32[40,128]{1,0:T(8,128)S(1)} %add.93), channel_id=1, source_target_pairs={{0,8},{8,0},{16,24},{24,16},{32,40},{40,32},{48,56},{56,48},{1,9},... | collective-permute-start | bytes 61448 | tf_op jit(solution)/shard_map/ppermute | solution.py:47
  140.3 5.3 %collective-permute-start.27 = (f32[40,128]{1,0:T(8,128)S(1)}, f32[40,128]{1,0:T(8,128)S(1)}, u32[]{:S(2)}, u32[]{:S(2)}) collective-permute-start(f32[40,128]{1,0:T(8,128)S(1)} %add.94), channel_id=1, source_target_pairs={{0,16},{8,24},{16,0},{24,8},{32,48},{40,56},{48,32},{56,40},{1,17}... | collective-permute-start | bytes 61448 | tf_op jit(solution)/shard_map/ppermute | solution.py:47
  145.6 5.3 %collective-permute-start.28 = (f32[40,128]{1,0:T(8,128)S(1)}, f32[40,128]{1,0:T(8,128)S(1)}, u32[]{:S(2)}, u32[]{:S(2)}) collective-permute-start(f32[40,128]{1,0:T(8,128)S(1)} %add.95), channel_id=1, source_target_pairs={{0,32},{8,40},{16,48},{24,56},{32,0},{40,8},{48,16},{56,24},{1,33}... | collective-permute-start | bytes 61448 | tf_op jit(solution)/shard_map/ppermute | solution.py:47
  150.9 3.8 %collective-permute-start.29 = (f32[40,128]{1,0:T(8,128)S(1)}, f32[40,128]{1,0:T(8,128)S(1)}, u32[]{:S(2)}, u32[]{:S(2)}) collective-permute-start(f32[40,128]{1,0:T(8,128)S(1)} %add.96), channel_id=1, source_target_pairs={{0,1},{1,0},{2,3},{3,2},{4,5},{5,4},{6,7},{7,6},{8,9},{9,8},{10,11... | collective-permute-start | bytes 61448 | tf_op jit(solution)/shard_map/ppermute | solution.py:47
  154.6 4.7 %collective-permute-start.30 = (f32[40,128]{1,0:T(8,128)S(1)}, f32[40,128]{1,0:T(8,128)S(1)}, u32[]{:S(2)}, u32[]{:S(2)}) collective-permute-start(f32[40,128]{1,0:T(8,128)S(1)} %add.97), channel_id=1, source_target_pairs={{0,2},{1,3},{2,0},{3,1},{4,6},{5,7},{6,4},{7,5},{8,10},{9,11},{10,... | collective-permute-start | bytes 61448 | tf_op jit(solution)/shard_map/ppermute | solution.py:47
  159.3 7.7 %collective-permute-start.31 = (f32[40,128]{1,0:T(8,128)S(1)}, f32[40,128]{1,0:T(8,128)S(1)}, u32[]{:S(2)}, u32[]{:S(2)}) collective-permute-start(f32[40,128]{1,0:T(8,128)S(1)} %add.98), channel_id=1, source_target_pairs={{0,4},{1,5},{2,6},{3,7},{4,0},{5,1},{6,2},{7,3},{8,12},{9,13},{10,... | collective-permute-start | bytes 61448 | tf_op jit(solution)/shard_map/ppermute | solution.py:47
  (1 other events, 0.7 us)

commit v2 on v1

--- a/solution.py
+++ b/solution.py
@@ -6,9 +6,11 @@
 from jax import lax
 from jax.experimental import pallas as pl
 from jax.experimental.pallas import tpu as pltpu
+from jax.sharding import Mesh
 from jax.sharding import PartitionSpec as P
 
 ITERS = 4
+AXES = (("y_low", "core"), ("y_high", "x"), "gz")
 CUTOFF = 10.0
 COULOMB = 0.3
 VOLUME = 10.0
@@ -24,6 +26,7 @@
 HOME = 13
 ROWS = 27 * TILES
 ENTRIES = 18
+LINES = 5
 
 VMEM = pl.BlockSpec(memory_space=pltpu.VMEM)
 SMEM = pl.BlockSpec(memory_space=pltpu.SMEM)
@@ -31,7 +34,7 @@
 
 def surrounded(cells):
     cells = cells[None]
-    for axis in ("gx", "gy", "gz"):
+    for axis in AXES:
         count = lax.axis_size(axis)
         before = lax.ppermute(cells, axis, [(i, (i + 1) % count) for i in range(count)])
         after = lax.ppermute(cells, axis, [((i + 1) % count, i) for i in range(count)])
@@ -39,13 +42,21 @@
     return cells
 
 
+def met(rows, axis, count, steps):
+    parts = [rows] + [
+        lax.ppermute(rows, axis, [(i, i ^ step) for i in range(count)]) for step in steps
+    ]
+    while len(parts) > 1:
+        parts = [parts[i] + parts[i + 1] for i in range(0, len(parts), 2)]
+    return parts[0]
+
+
 def summed(rows):
-    for axis in ("gx", "gy", "gz"):
-        count = lax.axis_size(axis)
-        step = 1
-        while step < count:
-            rows = rows + lax.ppermute(rows, axis, [(i, i ^ step) for i in range(count)])
-            step *= 2
+    rows = met(rows, "core", 2, (1,))
+    rows = met(rows, ("y_low", "y_high"), 4, (1, 2, 3))
+    rows = met(rows, "x", 4, (1, 2, 3))
+    for steps in ((1, 2, 3), (4,)):
+        rows = met(rows, "gz", 8, steps)
     return rows
 
 
@@ -130,7 +141,7 @@
             blocks[t, e] = (gap * gap) * (shape * shield)
             return carry
 
-        return lax.fori_loop(0, lists.shape[1], entry, carry, unroll=4)
+        return lax.fori_loop(0, lists.shape[1], entry, carry, unroll=36)
 
     lax.fori_loop(0, TILES, tile, 0)
 
@@ -156,23 +167,30 @@
     )(lists, far, powers, electro, near)
 
 
+def own_lanes():
+    shape = (LINES, 8, W)
+    return lax.broadcasted_iota(jnp.int32, shape, 2) // 16 == lax.broadcasted_iota(
+        jnp.int32, shape, 1
+    )
+
+
 def product_kernel(last, lists, scalars, around, kinds, blocks, *rest):
-    earlier, (out, total) = rest[:-2], rest[-2:]
+    earlier, (out, total, table) = rest[:-3], rest[-3:]
 
     def tile(t, carry):
         def entry(e, sums):
-            which = lists[t, e]
-            row = which // TILES * 16 + which % TILES
-            block = blocks[t, e]
-            return (
-                sums[0] + block * around[pl.ds(row, 1), :],
-                sums[1] + block * around[pl.ds(row + 8, 1), :],
+            at = lists[t, e]
+            block = blocks[t, e].reshape(W // 8, 8, W)
+            return tuple(
+                sums[k] + block * around[pl.ds(at + 8 * k, 8, stride=0), :][None]
+                for k in range(2)
             )
 
-        zero = jnp.zeros((W, W), F32)
-        sums = lax.fori_loop(0, lists.shape[1], entry, (zero, zero), unroll=2)
+        zero = jnp.zeros((W // 8, 8, W), F32)
+        sums = lax.fori_loop(0, lists.shape[1], entry, (zero, zero), unroll=12)
         for k in range(2):
-            total[pl.ds(t + 8 * k, 1), :] = jnp.sum(jnp.transpose(sums[k]), axis=0, keepdims=True)
+            turned = jnp.transpose(sums[k].reshape(W, W))
+            total[pl.ds(t + 8 * k, 1), :] = jnp.sum(turned, axis=0, keepdims=True)
         return carry
 
     lax.fori_loop(0, TILES, tile, 0)
@@ -188,18 +206,24 @@
         parts = [v[8 * k : 8 * k + 8] for v in basis]
         rows = [parts[i] * parts[j] for i in range(ITERS) for j in range(i, ITERS + 1)] + parts[:ITERS]
         for index, row in enumerate(rows):
-            out[2 * index + k : 2 * index + k + 1, :] = jnp.sum(row, axis=0, keepdims=True)
-    out[36:40, :] = jnp.zeros((4, W), F32)
+            table[2 * index + k : 2 * index + k + 1, :] = jnp.sum(row, axis=0, keepdims=True)
+    table[2 * ENTRIES :, :] = jnp.zeros((LINES * 8 - 2 * ENTRIES, W), F32)
+    folded = table[...]
+    for shift in (64, 32, 16):
+        folded = folded + pltpu.roll(folded, shift, 1)
+    kept = jnp.where(own_lanes(), folded.reshape(LINES, 8, W), 0.0)
+    out[:LINES, :] = jnp.sum(kept, axis=1)
+    out[LINES:, :] = jnp.zeros((8 - LINES, W), F32)
 
 
 def product(lists, scalars, around, kinds, blocks, earlier=()):
     last = bool(earlier)
     return pl.pallas_call(
         functools.partial(product_kernel, last),
-        out_shape=jax.ShapeDtypeStruct((40 if last else 16, W), F32),
+        out_shape=jax.ShapeDtypeStruct((8 if last else 16, W), F32),
         in_specs=[SMEM, SMEM, VMEM, VMEM, VMEM] + [VMEM] * len(earlier),
         out_specs=VMEM,
-        scratch_shapes=[pltpu.VMEM((16, W), F32)],
+        scratch_shapes=[pltpu.VMEM((16, W), F32), pltpu.VMEM((LINES * 8, W), F32)],
         compiler_params=pltpu.CompilerParams(vmem_limit_bytes=8 * MIB),
         name="product",
     )(lists, scalars, around, kinds, blocks, *earlier)
@@ -242,7 +266,9 @@
 
 
 def finish_kernel(scalars, gram, v0, v1, v2, v3, charges, solutions):
-    pair = (gram[...], jnp.zeros((40, W), F32))
+    spread_out = jnp.broadcast_to(gram[:LINES, :][:, None, :], (LINES, 8, W))
+    pair = (jnp.where(own_lanes(), spread_out, 0.0).reshape(LINES * 8, W),)
+    pair += (jnp.zeros((LINES * 8, W), F32),)
     shift = W // 2
     while shift:
         pair = add(pair, (pltpu.roll(pair[0], shift, 1), pltpu.roll(pair[1], shift, 1)))
@@ -300,7 +326,8 @@
         for i in range(1, ITERS):
             part = part + weights[i][0][k : k + 1] * basis[i][8 * k : 8 * k + 8]
         parts.append(part)
-        solutions[8 * k : 8 * k + 8, :] = part
+        for u in range(TILES):
+            solutions[u, k : k + 1, :] = part[u : u + 1]
     level = whole[0][0:1] / whole[0][1:2]
     charges[...] = parts[0] - level * parts[1]
 
@@ -308,7 +335,7 @@
 def finish(scalars, gram, basis):
     return pl.pallas_call(
         finish_kernel,
-        out_shape=(jax.ShapeDtypeStruct((TILES, W), F32), jax.ShapeDtypeStruct((16, W), F32)),
+        out_shape=(jax.ShapeDtypeStruct((TILES, W), F32), jax.ShapeDtypeStruct((TILES, 2, W), F32)),
         in_specs=[SMEM] + [VMEM] * 5,
         out_specs=(VMEM, VMEM),
         compiler_params=pltpu.CompilerParams(vmem_limit_bytes=8 * MIB),
@@ -322,8 +349,9 @@
     box = tile_lists // TILES
     place = (box % 3) * 9 + box // 3 % 3 * 3 + box // 9
     lists = place * TILES + tile_lists % TILES
+    rows = place * 2 * TILES + tile_lists % TILES
     inside = jnp.ones((27,), bool)
-    for k, axis in enumerate(("gx", "gy", "gz")):
+    for k, axis in enumerate(AXES):
         there = lax.axis_index(axis) + OFFSETS[:, k].astype(np.int32)
         inside = inside & (there >= 0) & (there < lax.axis_size(axis))
     far = jnp.where(inside, 0.0, FAR).astype(F32)
@@ -346,19 +374,21 @@
     basis = [start[16 * HOME : 16 * HOME + 16]]
     around = start
     for _ in range(ITERS - 1):
-        basis.append(product(lists, scalars, around, kinds, blocks))
+        basis.append(product(rows, scalars, around, kinds, blocks))
         around = surrounded(basis[-1]).reshape(27 * 16, W)
-    gram = summed(product(lists, scalars, around, kinds, blocks, tuple(basis[:-1])))
+    gram = summed(product(rows, scalars, around, kinds, blocks, tuple(basis[:-1])))
     charges, solutions = finish(scalars, gram, basis)
-    return charges.reshape(1, 1, 1, atoms), solutions.reshape(1, 1, 1, 2, atoms)
+    solutions = jnp.transpose(solutions, (1, 0, 2)).reshape(1, 1, 1, 2, atoms)
+    return charges.reshape(1, 1, 1, atoms), solutions
 
 
 def solution(mesh):
-    across = ("gx", "gy", "gz")
+    names = ("y_low", "core", "y_high", "x", "gz")
+    split = Mesh(mesh.devices.reshape(2, 2, 2, 4, mesh.shape["gz"]), names)
     return jax.shard_map(
         on_device,
-        mesh=mesh,
-        in_specs=(P(*across, None, None), P(*across, None), P(), P(), P(), P()),
-        out_specs=(P(*across, None), P(*across, None, None)),
+        mesh=split,
+        in_specs=(P(*AXES, None, None), P(*AXES, None), P(), P(), P(), P()),
+        out_specs=(P(*AXES, None), P(*AXES, None, None)),
         check_vma=False,
     )

time: 173 us -> 153 us (0.88); the launches traced: 170 us -> 153 us
  Pallas kernels: 54.3 us -> 38.4 us
  waiting for transfers between devices: 50.2 us -> 43.6 us
  starting transfers between devices: 53.4 us -> 58.6 us
    pallas_call x1, Pallas kernels: 24.3 us -> 16.1 us  [build(): pl.pallas_call(functools.partial(build_kernel, edge), out_shape=(pltpu.VM...]
    pallas_call x4, Pallas kernels: 27.6 us -> 19.9 us  [product(): pl.pallas_call(functools.partial(product_kernel, last), out_shape=jax.Sha...]
    ppermute x8 -> x11, waiting for transfers between devices: 23.1 us -> 16.6 us  [met(): lax.ppermute(rows, axis, [(i, i ^ step) for i in range(count)])]
    ppermute x8 -> x11, starting transfers between devices: 12.4 us -> 17.4 us  [met(): lax.ppermute(rows, axis, [(i, i ^ step) for i in range(count)])]
  transfers between devices with their start and end apart: 32 -> 35, of which waited for: 24 -> 25; matrix products, arithmetic and copies ran while one was open for 3% -> 4% of each run, Pallas kernels for 0% -> 0%
where the time goes in v2:
time: 153 us
  starting transfers between devices  58.6 us (38%)
  waiting for transfers between devices  43.6 us (28%)
  Pallas kernels  38.4 us (25%)
  other arithmetic  7.55 us (5%)
  between operations  3.68 us (2%)
    ppermute x12, starting transfers between devices, surrounded(): lax.ppermute(cells, axis, [((i + 1) % count, i) for i in range(count)])  32.2 us
    ppermute x12, waiting for transfers between devices, surrounded(): lax.ppermute(cells, axis, [(i, (i + 1) % count) for i in range(count)])  22.6 us
    pallas_call x4, Pallas kernels, product(): pl.pallas_call(functools.partial(product_kernel, last), out_shape=jax.Sha...  19.9 us
    ppermute x11, starting transfers between devices, met(): lax.ppermute(rows, axis, [(i, i ^ step) for i in range(count)])  17.4 us
    ppermute x11, waiting for transfers between devices, met(): lax.ppermute(rows, axis, [(i, i ^ step) for i in range(count)])  16.6 us
    pallas_call x1, Pallas kernels, build(): pl.pallas_call(functools.partial(build_kernel, edge), out_shape=(pltpu.VM...  16.1 us
    ppermute x12, starting transfers between devices, surrounded(): lax.ppermute(cells, axis, [(i, (i + 1) % count) for i in range(count)])  9.02 us
    ppermute x12, waiting for transfers between devices, surrounded(): lax.ppermute(cells, axis, [((i + 1) % count, i) for i in range(count)])  4.44 us
  transfers between devices with their start and end apart: 35, of which 25 were waited for; matrix products, arithmetic and copies ran while one was open for 4% of the time, Pallas kernels for 0%

profile of v2, /device:TPU:16, one launch (start us, length us, event | category | flops | bytes accessed | tf_op | source)
XLA Modules:
  0.0 152.8 jit_solution(4649722370960179350)
XLA Ops:
  11.2 4.2 %collective-permute-start.3 = (f32[3,32,128]{2,1,0:T(8,128)S(1)}, f32[3,32,128]{2,1,0:T(8,128)S(1)}, u32[]{:S(2)}, u32[]{:S(2)}) collective-permute-start(f32[3,32,128]{2,1,0:T(8,128)S(1)} %pad_maximum_fusion), channel_id=1, source_target_pairs={{8,0},{16,8},{24,16},{32,24},{40,32},{48,40},{56,48},{0,56},{9,1},... | collective-permute-start | bytes 147464 | tf_op jit(solution)/shard_map/ppermute | solution.py:40
  17.7 2.0 %collective-permute-start.4 = (f32[9,32,128]{2,1,0:T(8,128)S(1)}, f32[9,32,128]{2,1,0:T(8,128)S(1)}, u32[]{:S(2)}, u32[]{:S(2)}) collective-permute-start(f32[9,32,128]{2,1,0:T(8,128)S(1)} %constant_dynamic-update-slice_fusion), channel_id=1, source_target_pairs={{0,1},{1,2},{2,3},{3,4},{4,5},{5,6},{6,7},{7,0},{8,9},{9,10},{10,1... | collective-permute-start | bytes 442376 | tf_op jit(solution)/shard_map/ppermute | solution.py:39
  20.3 4.0 %collective-permute-start.5 = (f32[9,32,128]{2,1,0:T(8,128)S(1)}, f32[9,32,128]{2,1,0:T(8,128)S(1)}, u32[]{:S(2)}, u32[]{:S(2)}) collective-permute-start(f32[9,32,128]{2,1,0:T(8,128)S(1)} %constant_dynamic-update-slice_fusion), channel_id=1, source_target_pairs={{1,0},{2,1},{3,2},{4,3},{5,4},{6,5},{7,6},{0,7},{9,8},{10,9},{11,1... | collective-permute-start | bytes 442376 | tf_op jit(solution)/shard_map/ppermute | solution.py:40
  24.3 3.3 %collective-permute-done.4 = f32[9,32,128]{2,1,0:T(8,128)S(1)} collective-permute-done((f32[9,32,128]{2,1,0:T(8,128)S(1)}, f32[9,32,128]{2,1,0:T(8,128)S(1)}, u32[]{:S(2)}, u32[]{:S(2)}) %collective-permute-start.4) | collective-permute-done | bytes 147488 | tf_op jit(solution)/shard_map/ppermute | solution.py:39
  29.1 16.1 %build.1 = (f32[8,36,128,128]{3,2,1,0:T(8,128)S(1)}, f32[432,128]{1,0:T(8,128)S(1)}) custom-call(s32[8,36]{1,0:T(8,128)S(1)} %get-tuple-element.12.lists, f32[27]{0:T(128)S(1)} %and_select_fusion.far, f32[4]{0:T(128)S(1)} %power_multiply_fusion.powers, f32[4]{0:T(128)S(1)} %copy-done, f32[27,32,128]{2,1,0:T(8,128)S(1)} %constant_dynamic-update-slice_fusion.5.near), custom_call_target="tpu_custom_call" | custom-call | tf_op jit(solution)/shard_map/build/pallas_call | solution.py:151
  45.2 4.9 %product.4.rest_1_.v1 = f32[16,128]{1,0:T(8,128)S(1)} custom-call(s32[8,36]{1,0:T(8,128)S(1)} %multiply_add_fusion.1.lists, f32[8]{0:T(128)S(1)} %concatenate.50.scalars, f32[432,128]{1,0:T(8,128)S(1)} %get-tuple-element.6.around, f32[8,128]{1,0:T(8,128)S(1)} %bitcast.40, f32[8,36,128,128]{3,2,1,0:T(8,128)S(1)} %get-tuple-element.7.blocks), custom_call_target="tpu_custom_call" | custom-call | tf_op jit(solution)/shard_map/product/pallas_call | solution.py:221
  53.6 5.6 %collective-permute-start.9 = (f32[3,16,128]{2,1,0:T(8,128)S(1)}, f32[3,16,128]{2,1,0:T(8,128)S(1)}, u32[]{:S(2)}, u32[]{:S(2)}) collective-permute-start(f32[3,16,128]{2,1,0:T(8,128)S(1)} %pad_maximum_fusion.1), channel_id=1, source_target_pairs={{8,0},{16,8},{24,16},{32,24},{40,32},{48,40},{56,48},{0,56},{9,1},... | collective-permute-start | bytes 73736 | tf_op jit(solution)/shard_map/ppermute | solution.py:40
  59.2 1.8 %collective-permute-done.8 = f32[3,16,128]{2,1,0:T(8,128)S(1)} collective-permute-done((f32[3,16,128]{2,1,0:T(8,128)S(1)}, f32[3,16,128]{2,1,0:T(8,128)S(1)}, u32[]{:S(2)}, u32[]{:S(2)}) %collective-permute-start.8) | collective-permute-done | bytes 24608 | tf_op jit(solution)/shard_map/ppermute | solution.py:39
  61.2 3.2 %collective-permute-start.11 = (f32[9,16,128]{2,1,0:T(8,128)S(1)}, f32[9,16,128]{2,1,0:T(8,128)S(1)}, u32[]{:S(2)}, u32[]{:S(2)}) collective-permute-start(f32[9,16,128]{2,1,0:T(8,128)S(1)} %constant_dynamic-update-slice_fusion.12), channel_id=1, source_target_pairs={{1,0},{2,1},{3,2},{4,3},{5,4},{6,5},{7,6},{0,7},{9,8},{10,9},{11,1... | collective-permute-start | bytes 221192 | tf_op jit(solution)/shard_map/ppermute | solution.py:40
  64.4 2.3 %collective-permute-done.10 = f32[9,16,128]{2,1,0:T(8,128)S(1)} collective-permute-done((f32[9,16,128]{2,1,0:T(8,128)S(1)}, f32[9,16,128]{2,1,0:T(8,128)S(1)}, u32[]{:S(2)}, u32[]{:S(2)}) %collective-permute-start.10) | collective-permute-done | bytes 73760 | tf_op jit(solution)/shard_map/ppermute | solution.py:39
  66.8 4.9 %product.5.rest_2_.v2 = f32[16,128]{1,0:T(8,128)S(1)} custom-call(s32[8,36]{1,0:T(8,128)S(1)} %multiply_add_fusion.1.lists, f32[8]{0:T(128)S(1)} %concatenate.50.scalars, f32[432,128]{1,0:T(8,128)S(1)} %bitcast.28, f32[8,128]{1,0:T(8,128)S(1)} %bitcast.41, f32[8,36,128,128]{3,2,1,0:T(8,128)S(1)} %get-tuple-element.7.blocks), custom_call_target="tpu_custom_call" | custom-call | tf_op jit(solution)/shard_map/product/pallas_call | solution.py:221
  73.4 1.8 %collective-permute-done.12 = f32[1,16,128]{2,1,0:T(8,128)S(1)} collective-permute-done((f32[1,16,128]{2,1,0:T(8,128)S(1)}, f32[1,16,128]{2,1,0:T(8,128)S(1)}, u32[]{:S(2)}, u32[]{:S(2)}) %collective-permute-start.12) | collective-permute-done | bytes 8224 | tf_op jit(solution)/shard_map/ppermute | solution.py:39
  75.2 5.6 %collective-permute-start.15 = (f32[3,16,128]{2,1,0:T(8,128)S(1)}, f32[3,16,128]{2,1,0:T(8,128)S(1)}, u32[]{:S(2)}, u32[]{:S(2)}) collective-permute-start(f32[3,16,128]{2,1,0:T(8,128)S(1)} %pad_maximum_fusion.2), channel_id=1, source_target_pairs={{8,0},{16,8},{24,16},{32,24},{40,32},{48,40},{56,48},{0,56},{9,1},... | collective-permute-start | bytes 73736 | tf_op jit(solution)/shard_map/ppermute | solution.py:40
  80.8 1.8 %collective-permute-done.14 = f32[3,16,128]{2,1,0:T(8,128)S(1)} collective-permute-done((f32[3,16,128]{2,1,0:T(8,128)S(1)}, f32[3,16,128]{2,1,0:T(8,128)S(1)}, u32[]{:S(2)}, u32[]{:S(2)}) %collective-permute-start.14) | collective-permute-done | bytes 24608 | tf_op jit(solution)/shard_map/ppermute | solution.py:39
  82.6 2.1 %collective-permute-start.16 = (f32[9,16,128]{2,1,0:T(8,128)S(1)}, f32[9,16,128]{2,1,0:T(8,128)S(1)}, u32[]{:S(2)}, u32[]{:S(2)}) collective-permute-start(f32[9,16,128]{2,1,0:T(8,128)S(1)} %constant_dynamic-update-slice_fusion.24), channel_id=1, source_target_pairs={{0,1},{1,2},{2,3},{3,4},{4,5},{5,6},{6,7},{7,0},{8,9},{9,10},{10,1... | collective-permute-start | bytes 221192 | tf_op jit(solution)/shard_map/ppermute | solution.py:39
  85.9 2.3 %collective-permute-done.16 = f32[9,16,128]{2,1,0:T(8,128)S(1)} collective-permute-done((f32[9,16,128]{2,1,0:T(8,128)S(1)}, f32[9,16,128]{2,1,0:T(8,128)S(1)}, u32[]{:S(2)}, u32[]{:S(2)}) %collective-permute-start.16) | collective-permute-done | bytes 73760 | tf_op jit(solution)/shard_map/ppermute | solution.py:39
  89.1 4.9 %product.6.v3 = f32[16,128]{1,0:T(8,128)S(1)} custom-call(s32[8,36]{1,0:T(8,128)S(1)} %multiply_add_fusion.1.lists, f32[8]{0:T(128)S(1)} %concatenate.50.scalars, f32[432,128]{1,0:T(8,128)S(1)} %bitcast.29, f32[8,128]{1,0:T(8,128)S(1)} %bitcast.42, f32[8,36,128,128]{3,2,1,0:T(8,128)S(1)} %get-tuple-element.7.blocks), custom_call_target="tpu_custom_call" | custom-call | tf_op jit(solution)/shard_map/product/pallas_call | solution.py:221
  95.5 1.8 %collective-permute-done.18 = f32[1,16,128]{2,1,0:T(8,128)S(1)} collective-permute-done((f32[1,16,128]{2,1,0:T(8,128)S(1)}, f32[1,16,128]{2,1,0:T(8,128)S(1)}, u32[]{:S(2)}, u32[]{:S(2)}) %collective-permute-start.18) | collective-permute-done | bytes 8224 | tf_op jit(solution)/shard_map/ppermute | solution.py:39
  97.3 5.6 %collective-permute-start.21 = (f32[3,16,128]{2,1,0:T(8,128)S(1)}, f32[3,16,128]{2,1,0:T(8,128)S(1)}, u32[]{:S(2)}, u32[]{:S(2)}) collective-permute-start(f32[3,16,128]{2,1,0:T(8,128)S(1)} %pad_maximum_fusion.3), channel_id=1, source_target_pairs={{8,0},{16,8},{24,16},{32,24},{40,32},{48,40},{56,48},{0,56},{9,1},... | collective-permute-start | bytes 73736 | tf_op jit(solution)/shard_map/ppermute | solution.py:40
  102.9 1.8 %collective-permute-done.20 = f32[3,16,128]{2,1,0:T(8,128)S(1)} collective-permute-done((f32[3,16,128]{2,1,0:T(8,128)S(1)}, f32[3,16,128]{2,1,0:T(8,128)S(1)}, u32[]{:S(2)}, u32[]{:S(2)}) %collective-permute-start.20) | collective-permute-done | bytes 24608 | tf_op jit(solution)/shard_map/ppermute | solution.py:39
  104.7 2.1 %collective-permute-start.22 = (f32[9,16,128]{2,1,0:T(8,128)S(1)}, f32[9,16,128]{2,1,0:T(8,128)S(1)}, u32[]{:S(2)}, u32[]{:S(2)}) collective-permute-start(f32[9,16,128]{2,1,0:T(8,128)S(1)} %constant_dynamic-update-slice_fusion.36), channel_id=1, source_target_pairs={{0,1},{1,2},{2,3},{3,4},{4,5},{5,6},{6,7},{7,0},{8,9},{9,10},{10,1... | collective-permute-start | bytes 221192 | tf_op jit(solution)/shard_map/ppermute | solution.py:39
  108.1 2.3 %collective-permute-done.22 = f32[9,16,128]{2,1,0:T(8,128)S(1)} collective-permute-done((f32[9,16,128]{2,1,0:T(8,128)S(1)}, f32[9,16,128]{2,1,0:T(8,128)S(1)}, u32[]{:S(2)}, u32[]{:S(2)}) %collective-permute-start.22) | collective-permute-done | bytes 73760 | tf_op jit(solution)/shard_map/ppermute | solution.py:39
  111.2 5.1 %product.7 = f32[8,128]{1,0:T(8,128)S(1)} custom-call(s32[8,36]{1,0:T(8,128)S(1)} %multiply_add_fusion.1.lists, f32[8]{0:T(128)S(1)} %concatenate.50.scalars, f32[432,128]{1,0:T(8,128)S(1)} %bitcast.30, f32[8,128]{1,0:T(8,128)S(1)} %bitcast.43, f32[8,36,128,128]{3,2,1,0:T(8,128)S(1)} %get-tuple-element.7.blocks, f32[16,128]{1,0:T(8,128)S(1)} %slice.3.rest_0_.v0, ...), custom_call_target="tpu_custom_call" | custom-call | tf_op jit(solution)/shard_map/product/pallas_call | solution.py:221
  119.4 1.7 %collective-permute-start.25 = (f32[8,128]{1,0:T(8,128)S(1)}, f32[8,128]{1,0:T(8,128)S(1)}, u32[]{:S(2)}, u32[]{:S(2)}) collective-permute-start(f32[8,128]{1,0:T(8,128)S(1)} %add.115), channel_id=1, source_target_pairs={{0,32},{32,0},{128,160},{160,128},{1,33},{33,1},{129,161},{161,129... | collective-permute-start | bytes 12296 | tf_op jit(solution)/shard_map/ppermute | solution.py:47
  121.6 2.9 %collective-permute-done.25 = f32[8,128]{1,0:T(8,128)S(1)} collective-permute-done((f32[8,128]{1,0:T(8,128)S(1)}, f32[8,128]{1,0:T(8,128)S(1)}, u32[]{:S(2)}, u32[]{:S(2)}) %collective-permute-start.25) | collective-permute-done | bytes 4128 | tf_op jit(solution)/shard_map/ppermute | solution.py:47
  124.5 5.5 %collective-permute-start.30 = (f32[8,128]{1,0:T(8,128)S(1)}, f32[8,128]{1,0:T(8,128)S(1)}, u32[]{:S(2)}, u32[]{:S(2)}) collective-permute-start(f32[8,128]{1,0:T(8,128)S(1)} %add_add_fusion.2), channel_id=1, source_target_pairs={{0,24},{8,16},{16,8},{24,0},{1,25},{9,17},{17,9},{25,1},{2,26},{10... | collective-permute-start | bytes 12296 | tf_op jit(solution)/shard_map/ppermute | solution.py:47
  131.6 3.5 %collective-permute-done.29 = f32[8,128]{1,0:T(8,128)S(1)} collective-permute-done((f32[8,128]{1,0:T(8,128)S(1)}, f32[8,128]{1,0:T(8,128)S(1)}, u32[]{:S(2)}, u32[]{:S(2)}) %collective-permute-start.29) | collective-permute-done | bytes 4128 | tf_op jit(solution)/shard_map/ppermute | solution.py:47
  135.1 3.2 %collective-permute-start.33 = (f32[8,128]{1,0:T(8,128)S(1)}, f32[8,128]{1,0:T(8,128)S(1)}, u32[]{:S(2)}, u32[]{:S(2)}) collective-permute-start(f32[8,128]{1,0:T(8,128)S(1)} %add_add_fusion.1), channel_id=1, source_target_pairs={{0,3},{1,2},{2,1},{3,0},{4,7},{5,6},{6,5},{7,4},{8,11},{9,10},{10,... | collective-permute-start | bytes 12296 | tf_op jit(solution)/shard_map/ppermute | solution.py:47
  140.6 2.2 %collective-permute-done.32 = f32[8,128]{1,0:T(8,128)S(1)} collective-permute-done((f32[8,128]{1,0:T(8,128)S(1)}, f32[8,128]{1,0:T(8,128)S(1)}, u32[]{:S(2)}, u32[]{:S(2)}) %collective-permute-start.32) | collective-permute-done | bytes 4128 | tf_op jit(solution)/shard_map/ppermute | solution.py:47
  142.8 2.7 %collective-permute-start.34 = (f32[8,128]{1,0:T(8,128)S(1)}, f32[8,128]{1,0:T(8,128)S(1)}, u32[]{:S(2)}, u32[]{:S(2)}) collective-permute-start(f32[8,128]{1,0:T(8,128)S(1)} %add_add_fusion), channel_id=1, source_target_pairs={{0,4},{1,5},{2,6},{3,7},{4,0},{5,1},{6,2},{7,3},{8,12},{9,13},{10,... | collective-permute-start | bytes 12296 | tf_op jit(solution)/shard_map/ppermute | solution.py:47
  145.5 4.9 %collective-permute-done.34 = f32[8,128]{1,0:T(8,128)S(1)} collective-permute-done((f32[8,128]{1,0:T(8,128)S(1)}, f32[8,128]{1,0:T(8,128)S(1)}, u32[]{:S(2)}, u32[]{:S(2)}) %collective-permute-start.34) | collective-permute-done | bytes 4128 | tf_op jit(solution)/shard_map/ppermute | solution.py:47
  150.4 2.4 %finish.1 = (f32[8,128]{1,0:T(8,128)}, f32[8,2,128]{2,1,0:T(2,128)}) custom-call(f32[8]{0:T(128)S(1)} %concatenate.50.scalars, f32[8,128]{1,0:T(8,128)S(1)} %add.125.gram, f32[16,128]{1,0:T(8,128)S(1)} %slice.3.rest_0_.v0, f32[16,128]{1,0:T(8,128)S(1)} %product.4.rest_1_.v1, f32[16,128]{1,0:T(8,128)S(1)} %product.5.rest_2_.v2, f32[16,128]{1,0:T(8,128)S(1)} %product.6.v3), custom_call_target="tpu_custom_call" | custom-call | tf_op jit(solution)/shard_map/finish/pallas_call | solution.py:336
  (113 shorter events, 30.4 us)
Async XLA Ops:
  2.0 6.7 %collective-permute-start.1 = (f32[1,32,128]{2,1,0:T(8,128)S(1)}, f32[1,32,128]{2,1,0:T(8,128)S(1)}, u32[]{:S(2)}, u32[]{:S(2)}) collective-permute-start(f32[1,32,128]{2,1,0:T(8,128)S(1)} %maximum_bitcast_fusion), channel_id=1, source_target_pairs={{64,0},{128,64},{192,128},{0,192},{65,1},{129,65},{193,129},{1,193... | collective-permute-start | bytes 49160 | tf_op jit(solution)/shard_map/ppermute | solution.py:40
  2.8 6.0 %collective-permute-start = (f32[1,32,128]{2,1,0:T(8,128)S(1)}, f32[1,32,128]{2,1,0:T(8,128)S(1)}, u32[]{:S(2)}, u32[]{:S(2)}) collective-permute-start(f32[1,32,128]{2,1,0:T(8,128)S(1)} %maximum_bitcast_fusion), channel_id=1, source_target_pairs={{0,64},{64,128},{128,192},{192,0},{1,65},{65,129},{129,193},{193,1... | collective-permute-start | bytes 49160 | tf_op jit(solution)/shard_map/ppermute | solution.py:39
  8.8 8.2 %collective-permute-start.2 = (f32[3,32,128]{2,1,0:T(8,128)S(1)}, f32[3,32,128]{2,1,0:T(8,128)S(1)}, u32[]{:S(2)}, u32[]{:S(2)}) collective-permute-start(f32[3,32,128]{2,1,0:T(8,128)S(1)} %pad_maximum_fusion), channel_id=1, source_target_pairs={{0,8},{8,16},{16,24},{24,32},{32,40},{40,48},{48,56},{56,0},{1,9},... | collective-permute-start | bytes 147464 | tf_op jit(solution)/shard_map/ppermute | solution.py:39
  11.2 6.5 %collective-permute-start.3 = (f32[3,32,128]{2,1,0:T(8,128)S(1)}, f32[3,32,128]{2,1,0:T(8,128)S(1)}, u32[]{:S(2)}, u32[]{:S(2)}) collective-permute-start(f32[3,32,128]{2,1,0:T(8,128)S(1)} %pad_maximum_fusion), channel_id=1, source_target_pairs={{8,0},{16,8},{24,16},{32,24},{40,32},{48,40},{56,48},{0,56},{9,1},... | collective-permute-start | bytes 147464 | tf_op jit(solution)/shard_map/ppermute | solution.py:40
  17.7 9.9 %collective-permute-start.4 = (f32[9,32,128]{2,1,0:T(8,128)S(1)}, f32[9,32,128]{2,1,0:T(8,128)S(1)}, u32[]{:S(2)}, u32[]{:S(2)}) collective-permute-start(f32[9,32,128]{2,1,0:T(8,128)S(1)} %constant_dynamic-update-slice_fusion), channel_id=1, source_target_pairs={{0,1},{1,2},{2,3},{3,4},{4,5},{5,6},{6,7},{7,0},{8,9},{9,10},{10,1... | collective-permute-start | bytes 442376 | tf_op jit(solution)/shard_map/ppermute | solution.py:39
  20.3 8.1 %collective-permute-start.5 = (f32[9,32,128]{2,1,0:T(8,128)S(1)}, f32[9,32,128]{2,1,0:T(8,128)S(1)}, u32[]{:S(2)}, u32[]{:S(2)}) collective-permute-start(f32[9,32,128]{2,1,0:T(8,128)S(1)} %constant_dynamic-update-slice_fusion), channel_id=1, source_target_pairs={{1,0},{2,1},{3,2},{4,3},{5,4},{6,5},{7,6},{0,7},{9,8},{10,9},{11,1... | collective-permute-start | bytes 442376 | tf_op jit(solution)/shard_map/ppermute | solution.py:40
  50.1 1.8 %collective-permute-start.7 = (f32[1,16,128]{2,1,0:T(8,128)S(1)}, f32[1,16,128]{2,1,0:T(8,128)S(1)}, u32[]{:S(2)}, u32[]{:S(2)}) collective-permute-start(f32[1,16,128]{2,1,0:T(8,128)S(1)} %bitcast.31), channel_id=1, source_target_pairs={{64,0},{128,64},{192,128},{0,192},{65,1},{129,65},{193,129},{1,193... | collective-permute-start | bytes 24584 | tf_op jit(solution)/shard_map/ppermute | solution.py:40
  50.5 3.1 %collective-permute-start.6 = (f32[1,16,128]{2,1,0:T(8,128)S(1)}, f32[1,16,128]{2,1,0:T(8,128)S(1)}, u32[]{:S(2)}, u32[]{:S(2)}) collective-permute-start(f32[1,16,128]{2,1,0:T(8,128)S(1)} %bitcast.32), channel_id=1, source_target_pairs={{0,64},{64,128},{128,192},{192,0},{1,65},{65,129},{129,193},{193,1... | collective-permute-start | bytes 24584 | tf_op jit(solution)/shard_map/ppermute | solution.py:39
  53.6 7.4 %collective-permute-start.8 = (f32[3,16,128]{2,1,0:T(8,128)S(1)}, f32[3,16,128]{2,1,0:T(8,128)S(1)}, u32[]{:S(2)}, u32[]{:S(2)}) collective-permute-start(f32[3,16,128]{2,1,0:T(8,128)S(1)} %pad_maximum_fusion.1), channel_id=1, source_target_pairs={{0,8},{8,16},{16,24},{24,32},{32,40},{40,48},{48,56},{56,0},{1,9},... | collective-permute-start | bytes 73736 | tf_op jit(solution)/shard_map/ppermute | solution.py:39
  53.6 7.5 %collective-permute-start.9 = (f32[3,16,128]{2,1,0:T(8,128)S(1)}, f32[3,16,128]{2,1,0:T(8,128)S(1)}, u32[]{:S(2)}, u32[]{:S(2)}) collective-permute-start(f32[3,16,128]{2,1,0:T(8,128)S(1)} %pad_maximum_fusion.1), channel_id=1, source_target_pairs={{8,0},{16,8},{24,16},{32,24},{40,32},{48,40},{56,48},{0,56},{9,1},... | collective-permute-start | bytes 73736 | tf_op jit(solution)/shard_map/ppermute | solution.py:40
  61.1 5.6 %collective-permute-start.10 = (f32[9,16,128]{2,1,0:T(8,128)S(1)}, f32[9,16,128]{2,1,0:T(8,128)S(1)}, u32[]{:S(2)}, u32[]{:S(2)}) collective-permute-start(f32[9,16,128]{2,1,0:T(8,128)S(1)} %constant_dynamic-update-slice_fusion.12), channel_id=1, source_target_pairs={{0,1},{1,2},{2,3},{3,4},{4,5},{5,6},{6,7},{7,0},{8,9},{9,10},{10,1... | collective-permute-start | bytes 221192 | tf_op jit(solution)/shard_map/ppermute | solution.py:39
  61.2 5.6 %collective-permute-start.11 = (f32[9,16,128]{2,1,0:T(8,128)S(1)}, f32[9,16,128]{2,1,0:T(8,128)S(1)}, u32[]{:S(2)}, u32[]{:S(2)}) collective-permute-start(f32[9,16,128]{2,1,0:T(8,128)S(1)} %constant_dynamic-update-slice_fusion.12), channel_id=1, source_target_pairs={{1,0},{2,1},{3,2},{4,3},{5,4},{6,5},{7,6},{0,7},{9,8},{10,9},{11,1... | collective-permute-start | bytes 221192 | tf_op jit(solution)/shard_map/ppermute | solution.py:40
  72.0 3.2 %collective-permute-start.12 = (f32[1,16,128]{2,1,0:T(8,128)S(1)}, f32[1,16,128]{2,1,0:T(8,128)S(1)}, u32[]{:S(2)}, u32[]{:S(2)}) collective-permute-start(f32[1,16,128]{2,1,0:T(8,128)S(1)} %bitcast.35), channel_id=1, source_target_pairs={{0,64},{64,128},{128,192},{192,0},{1,65},{65,129},{129,193},{193,1... | collective-permute-start | bytes 24584 | tf_op jit(solution)/shard_map/ppermute | solution.py:39
  75.2 7.4 %collective-permute-start.14 = (f32[3,16,128]{2,1,0:T(8,128)S(1)}, f32[3,16,128]{2,1,0:T(8,128)S(1)}, u32[]{:S(2)}, u32[]{:S(2)}) collective-permute-start(f32[3,16,128]{2,1,0:T(8,128)S(1)} %pad_maximum_fusion.2), channel_id=1, source_target_pairs={{0,8},{8,16},{16,24},{24,32},{32,40},{40,48},{48,56},{56,0},{1,9},... | collective-permute-start | bytes 73736 | tf_op jit(solution)/shard_map/ppermute | solution.py:39
  75.2 7.5 %collective-permute-start.15 = (f32[3,16,128]{2,1,0:T(8,128)S(1)}, f32[3,16,128]{2,1,0:T(8,128)S(1)}, u32[]{:S(2)}, u32[]{:S(2)}) collective-permute-start(f32[3,16,128]{2,1,0:T(8,128)S(1)} %pad_maximum_fusion.2), channel_id=1, source_target_pairs={{8,0},{16,8},{24,16},{32,24},{40,32},{48,40},{56,48},{0,56},{9,1},... | collective-permute-start | bytes 73736 | tf_op jit(solution)/shard_map/ppermute | solution.py:40
  82.6 5.6 %collective-permute-start.16 = (f32[9,16,128]{2,1,0:T(8,128)S(1)}, f32[9,16,128]{2,1,0:T(8,128)S(1)}, u32[]{:S(2)}, u32[]{:S(2)}) collective-permute-start(f32[9,16,128]{2,1,0:T(8,128)S(1)} %constant_dynamic-update-slice_fusion.24), channel_id=1, source_target_pairs={{0,1},{1,2},{2,3},{3,4},{4,5},{5,6},{6,7},{7,0},{8,9},{9,10},{10,1... | collective-permute-start | bytes 221192 | tf_op jit(solution)/shard_map/ppermute | solution.py:39
  84.7 4.4 %collective-permute-start.17 = (f32[9,16,128]{2,1,0:T(8,128)S(1)}, f32[9,16,128]{2,1,0:T(8,128)S(1)}, u32[]{:S(2)}, u32[]{:S(2)}) collective-permute-start(f32[9,16,128]{2,1,0:T(8,128)S(1)} %constant_dynamic-update-slice_fusion.24), channel_id=1, source_target_pairs={{1,0},{2,1},{3,2},{4,3},{5,4},{6,5},{7,6},{0,7},{9,8},{10,9},{11,1... | collective-permute-start | bytes 221192 | tf_op jit(solution)/shard_map/ppermute | solution.py:40
  94.1 3.2 %collective-permute-start.18 = (f32[1,16,128]{2,1,0:T(8,128)S(1)}, f32[1,16,128]{2,1,0:T(8,128)S(1)}, u32[]{:S(2)}, u32[]{:S(2)}) collective-permute-start(f32[1,16,128]{2,1,0:T(8,128)S(1)} %bitcast.45), channel_id=1, source_target_pairs={{0,64},{64,128},{128,192},{192,0},{1,65},{65,129},{129,193},{193,1... | collective-permute-start | bytes 24584 | tf_op jit(solution)/shard_map/ppermute | solution.py:39
  97.3 7.4 %collective-permute-start.20 = (f32[3,16,128]{2,1,0:T(8,128)S(1)}, f32[3,16,128]{2,1,0:T(8,128)S(1)}, u32[]{:S(2)}, u32[]{:S(2)}) collective-permute-start(f32[3,16,128]{2,1,0:T(8,128)S(1)} %pad_maximum_fusion.3), channel_id=1, source_target_pairs={{0,8},{8,16},{16,24},{24,32},{32,40},{40,48},{48,56},{56,0},{1,9},... | collective-permute-start | bytes 73736 | tf_op jit(solution)/shard_map/ppermute | solution.py:39
  97.3 7.5 %collective-permute-start.21 = (f32[3,16,128]{2,1,0:T(8,128)S(1)}, f32[3,16,128]{2,1,0:T(8,128)S(1)}, u32[]{:S(2)}, u32[]{:S(2)}) collective-permute-start(f32[3,16,128]{2,1,0:T(8,128)S(1)} %pad_maximum_fusion.3), channel_id=1, source_target_pairs={{8,0},{16,8},{24,16},{32,24},{40,32},{48,40},{56,48},{0,56},{9,1},... | collective-permute-start | bytes 73736 | tf_op jit(solution)/shard_map/ppermute | solution.py:40
  104.7 5.6 %collective-permute-start.22 = (f32[9,16,128]{2,1,0:T(8,128)S(1)}, f32[9,16,128]{2,1,0:T(8,128)S(1)}, u32[]{:S(2)}, u32[]{:S(2)}) collective-permute-start(f32[9,16,128]{2,1,0:T(8,128)S(1)} %constant_dynamic-update-slice_fusion.36), channel_id=1, source_target_pairs={{0,1},{1,2},{2,3},{3,4},{4,5},{5,6},{6,7},{7,0},{8,9},{9,10},{10,1... | collective-permute-start | bytes 221192 | tf_op jit(solution)/shard_map/ppermute | solution.py:39
  106.8 4.4 %collective-permute-start.23 = (f32[9,16,128]{2,1,0:T(8,128)S(1)}, f32[9,16,128]{2,1,0:T(8,128)S(1)}, u32[]{:S(2)}, u32[]{:S(2)}) collective-permute-start(f32[9,16,128]{2,1,0:T(8,128)S(1)} %constant_dynamic-update-slice_fusion.36), channel_id=1, source_target_pairs={{1,0},{2,1},{3,2},{4,3},{5,4},{6,5},{7,6},{0,7},{9,8},{10,9},{11,1... | collective-permute-start | bytes 221192 | tf_op jit(solution)/shard_map/ppermute | solution.py:40
  117.6 3.6 %collective-permute-start.27 = (f32[8,128]{1,0:T(8,128)S(1)}, f32[8,128]{1,0:T(8,128)S(1)}, u32[]{:S(2)}, u32[]{:S(2)}) collective-permute-start(f32[8,128]{1,0:T(8,128)S(1)} %add.115), channel_id=1, source_target_pairs={{0,160},{32,128},{128,32},{160,0},{1,161},{33,129},{129,33},{161,1... | collective-permute-start | bytes 12296 | tf_op jit(solution)/shard_map/ppermute | solution.py:47
  118.0 3.6 %collective-permute-start.26 = (f32[8,128]{1,0:T(8,128)S(1)}, f32[8,128]{1,0:T(8,128)S(1)}, u32[]{:S(2)}, u32[]{:S(2)}) collective-permute-start(f32[8,128]{1,0:T(8,128)S(1)} %add.115), channel_id=1, source_target_pairs={{0,128},{32,160},{128,0},{160,32},{1,129},{33,161},{129,1},{161,33... | collective-permute-start | bytes 12296 | tf_op jit(solution)/shard_map/ppermute | solution.py:47
  119.4 5.1 %collective-permute-start.25 = (f32[8,128]{1,0:T(8,128)S(1)}, f32[8,128]{1,0:T(8,128)S(1)}, u32[]{:S(2)}, u32[]{:S(2)}) collective-permute-start(f32[8,128]{1,0:T(8,128)S(1)} %add.115), channel_id=1, source_target_pairs={{0,32},{32,0},{128,160},{160,128},{1,33},{33,1},{129,161},{161,129... | collective-permute-start | bytes 12296 | tf_op jit(solution)/shard_map/ppermute | solution.py:47
  124.5 7.1 %collective-permute-start.30 = (f32[8,128]{1,0:T(8,128)S(1)}, f32[8,128]{1,0:T(8,128)S(1)}, u32[]{:S(2)}, u32[]{:S(2)}) collective-permute-start(f32[8,128]{1,0:T(8,128)S(1)} %add_add_fusion.2), channel_id=1, source_target_pairs={{0,24},{8,16},{16,8},{24,0},{1,25},{9,17},{17,9},{25,1},{2,26},{10... | collective-permute-start | bytes 12296 | tf_op jit(solution)/shard_map/ppermute | solution.py:47
  130.0 5.1 %collective-permute-start.29 = (f32[8,128]{1,0:T(8,128)S(1)}, f32[8,128]{1,0:T(8,128)S(1)}, u32[]{:S(2)}, u32[]{:S(2)}) collective-permute-start(f32[8,128]{1,0:T(8,128)S(1)} %add_add_fusion.2), channel_id=1, source_target_pairs={{0,16},{8,24},{16,0},{24,8},{1,17},{9,25},{17,1},{25,9},{2,18},{10... | collective-permute-start | bytes 12296 | tf_op jit(solution)/shard_map/ppermute | solution.py:47
  130.0 5.1 %collective-permute-start.28 = (f32[8,128]{1,0:T(8,128)S(1)}, f32[8,128]{1,0:T(8,128)S(1)}, u32[]{:S(2)}, u32[]{:S(2)}) collective-permute-start(f32[8,128]{1,0:T(8,128)S(1)} %add_add_fusion.2), channel_id=1, source_target_pairs={{0,8},{8,0},{16,24},{24,16},{1,9},{9,1},{17,25},{25,17},{2,10},{10... | collective-permute-start | bytes 12296 | tf_op jit(solution)/shard_map/ppermute | solution.py:47
  135.1 5.5 %collective-permute-start.33 = (f32[8,128]{1,0:T(8,128)S(1)}, f32[8,128]{1,0:T(8,128)S(1)}, u32[]{:S(2)}, u32[]{:S(2)}) collective-permute-start(f32[8,128]{1,0:T(8,128)S(1)} %add_add_fusion.1), channel_id=1, source_target_pairs={{0,3},{1,2},{2,1},{3,0},{4,7},{5,6},{6,5},{7,4},{8,11},{9,10},{10,... | collective-permute-start | bytes 12296 | tf_op jit(solution)/shard_map/ppermute | solution.py:47
  138.3 4.5 %collective-permute-start.32 = (f32[8,128]{1,0:T(8,128)S(1)}, f32[8,128]{1,0:T(8,128)S(1)}, u32[]{:S(2)}, u32[]{:S(2)}) collective-permute-start(f32[8,128]{1,0:T(8,128)S(1)} %add_add_fusion.1), channel_id=1, source_target_pairs={{0,2},{1,3},{2,0},{3,1},{4,6},{5,7},{6,4},{7,5},{8,10},{9,11},{10,... | collective-permute-start | bytes 12296 | tf_op jit(solution)/shard_map/ppermute | solution.py:47
  138.3 4.5 %collective-permute-start.31 = (f32[8,128]{1,0:T(8,128)S(1)}, f32[8,128]{1,0:T(8,128)S(1)}, u32[]{:S(2)}, u32[]{:S(2)}) collective-permute-start(f32[8,128]{1,0:T(8,128)S(1)} %add_add_fusion.1), channel_id=1, source_target_pairs={{0,1},{1,0},{2,3},{3,2},{4,5},{5,4},{6,7},{7,6},{8,9},{9,8},{10,11... | collective-permute-start | bytes 12296 | tf_op jit(solution)/shard_map/ppermute | solution.py:47
  142.8 7.6 %collective-permute-start.34 = (f32[8,128]{1,0:T(8,128)S(1)}, f32[8,128]{1,0:T(8,128)S(1)}, u32[]{:S(2)}, u32[]{:S(2)}) collective-permute-start(f32[8,128]{1,0:T(8,128)S(1)} %add_add_fusion), channel_id=1, source_target_pairs={{0,4},{1,5},{2,6},{3,7},{4,0},{5,1},{6,2},{7,3},{8,12},{9,13},{10,... | collective-permute-start | bytes 12296 | tf_op jit(solution)/shard_map/ppermute | solution.py:47
  (4 other events, 5.0 us)

commit v3 on v2

--- a/solution.py
+++ b/solution.py
@@ -75,7 +75,7 @@
     )
 
 
-def build_kernel(edge, lists, far, powers, electro, near, blocks, start, others, others_p, own, floor):
+def build_kernel(edge, lists, far, table, near, blocks, start, others, others_p, own, floor):
     zero = jnp.zeros((TILES, W), F32)
     one = jnp.ones((TILES, W), F32)
 
@@ -86,7 +86,9 @@
         ]
         kind = near[box, 24:32, :]
         square = place[0] * place[0] + place[1] * place[1] + place[2] * place[2]
-        return place, kind, by_kind(kind, powers), square
+        root = lax.rsqrt(by_kind(kind, [table[8 + k] for k in range(4)]))
+        power = root * root * root * CUTOFF**-1.5
+        return place, kind, power, square
 
     for box in range(27):
         place, kind, power, square = atoms(box)
@@ -100,7 +102,7 @@
         high, middle, _ = pieces(power)
         for k, row in enumerate([high, middle, high] + [zero] * 5):
             others_p[k * ROWS + box * 8 : k * ROWS + box * 8 + 8, :] = row
-        start[16 * box : 16 * box + 8, :] = -by_kind(kind, electro)
+        start[16 * box : 16 * box + 8, :] = -by_kind(kind, [table[4 + k] for k in range(4)])
         start[16 * box + 8 : 16 * box + 16, :] = -one
     place, kind, power, square = atoms(HOME)
     rows = []
@@ -123,7 +125,8 @@
         left = jnp.transpose(own[pl.ds(t, W, stride=8), :])[:, :32].astype(BF16)
 
         def entry(e, carry):
-            which = lists[t, e]
+            row = lists[t, e]
+            which = (row >> 4) * TILES + (row & 7)
             right = others[pl.ds(which, 32, stride=ROWS), :].astype(BF16)
             right_p = others_p[pl.ds(which, 8, stride=ROWS), :].astype(BF16)
             right = jnp.concatenate([right, jnp.concatenate([blank, right_p], axis=0)], axis=1)
@@ -146,7 +149,7 @@
     lax.fori_loop(0, TILES, tile, 0)
 
 
-def build(lists, far, powers, electro, near, edge):
+def build(lists, far, table, near, edge):
     entries = lists.shape[1]
     return pl.pallas_call(
         functools.partial(build_kernel, edge),
@@ -154,7 +157,7 @@
             pltpu.VMEM((TILES, entries, W, W), F32),
             jax.ShapeDtypeStruct((27 * 16, W), F32),
         ),
-        in_specs=[SMEM, SMEM, SMEM, SMEM, VMEM],
+        in_specs=[SMEM, SMEM, SMEM, VMEM],
         out_specs=(VMEM, VMEM),
         scratch_shapes=[
             pltpu.VMEM((32 * ROWS, W), F32),
@@ -164,7 +167,14 @@
         ],
         compiler_params=pltpu.CompilerParams(vmem_limit_bytes=8 * MIB),
         name="build",
-    )(lists, far, powers, electro, near)
+    )(lists, far, table, near)
+
+
+def spectrum(table, shape):
+    values = [jnp.full(shape, table[k], F32) for k in range(4)]
+    least = jnp.minimum(jnp.minimum(values[0], values[1]), jnp.minimum(values[2], values[3]))
+    most = jnp.maximum(jnp.maximum(values[0], values[1]), jnp.maximum(values[2], values[3]))
+    return 0.5 * (least + most) + 1.0, 0.5 * (most - least) + 1.5
 
 
 def own_lanes():
@@ -174,8 +184,8 @@
     )
 
 
-def product_kernel(last, lists, scalars, around, kinds, blocks, *rest):
-    earlier, (out, total, table) = rest[:-3], rest[-3:]
+def product_kernel(last, lists, table, around, kinds, blocks, *rest):
+    earlier, (out, total, dots) = rest[:-3], rest[-3:]
 
     def tile(t, carry):
         def entry(e, sums):
@@ -195,9 +205,13 @@
 
     lax.fori_loop(0, TILES, tile, 0)
     kind = kinds[...]
-    eta = by_kind(kind, [scalars[2 + k] for k in range(4)])
+    centre, spread = spectrum(table, (TILES, W))
+    eta = by_kind(kind, [table[k] for k in range(4)]) - centre
     home = around[16 * HOME : 16 * HOME + 16, :]
-    following = total[...] * scalars[0] + jnp.concatenate([eta, eta], axis=0) * home
+    scale = 20.0 * COULOMB / CUTOFF
+    following = (total[...] * scale + jnp.concatenate([eta, eta], axis=0) * home) / (
+        jnp.concatenate([spread, spread], axis=0)
+    )
     if not last:
         out[...] = following
         return
@@ -206,9 +220,9 @@
         parts = [v[8 * k : 8 * k + 8] for v in basis]
         rows = [parts[i] * parts[j] for i in range(ITERS) for j in range(i, ITERS + 1)] + parts[:ITERS]
         for index, row in enumerate(rows):
-            table[2 * index + k : 2 * index + k + 1, :] = jnp.sum(row, axis=0, keepdims=True)
-    table[2 * ENTRIES :, :] = jnp.zeros((LINES * 8 - 2 * ENTRIES, W), F32)
-    folded = table[...]
+            dots[2 * index + k : 2 * index + k + 1, :] = jnp.sum(row, axis=0, keepdims=True)
+    dots[2 * ENTRIES :, :] = jnp.zeros((LINES * 8 - 2 * ENTRIES, W), F32)
+    folded = dots[...]
     for shift in (64, 32, 16):
         folded = folded + pltpu.roll(folded, shift, 1)
     kept = jnp.where(own_lanes(), folded.reshape(LINES, 8, W), 0.0)
@@ -216,7 +230,7 @@
     out[LINES:, :] = jnp.zeros((8 - LINES, W), F32)
 
 
-def product(lists, scalars, around, kinds, blocks, earlier=()):
+def product(lists, table, around, kinds, blocks, earlier=()):
     last = bool(earlier)
     return pl.pallas_call(
         functools.partial(product_kernel, last),
@@ -226,7 +240,7 @@
         scratch_shapes=[pltpu.VMEM((16, W), F32), pltpu.VMEM((LINES * 8, W), F32)],
         compiler_params=pltpu.CompilerParams(vmem_limit_bytes=8 * MIB),
         name="product",
-    )(lists, scalars, around, kinds, blocks, *earlier)
+    )(lists, table, around, kinds, blocks, *earlier)
 
 
 def two_sum(a, b):
@@ -265,7 +279,7 @@
     return add(guess, mul(guess, slip))
 
 
-def finish_kernel(scalars, gram, v0, v1, v2, v3, charges, solutions):
+def finish_kernel(table, gram, v0, v1, v2, v3, charges, solutions):
     spread_out = jnp.broadcast_to(gram[:LINES, :][:, None, :], (LINES, 8, W))
     pair = (jnp.where(own_lanes(), spread_out, 0.0).reshape(LINES * 8, W),)
     pair += (jnp.zeros((LINES * 8, W), F32),)
@@ -288,8 +302,7 @@
         return dots[min(i, j), max(i, j)]
 
     none = jnp.zeros((2, W), F32)
-    spread = (jnp.full((2, W), scalars[6], F32), none)
-    centre = (jnp.full((2, W), scalars[7], F32), none)
+    centre, spread = ((value, none) for value in spectrum(table, (2, W)))
     matrix = {
         (i, j): add(mul(spread, dot(i, j + 1)), mul(centre, dot(i, j)))
         for i in range(ITERS)
@@ -332,7 +345,7 @@
     charges[...] = parts[0] - level * parts[1]
 
 
-def finish(scalars, gram, basis):
+def finish(table, gram, basis):
     return pl.pallas_call(
         finish_kernel,
         out_shape=(jax.ShapeDtypeStruct((TILES, W), F32), jax.ShapeDtypeStruct((TILES, 2, W), F32)),
@@ -340,7 +353,7 @@
         out_specs=(VMEM, VMEM),
         compiler_params=pltpu.CompilerParams(vmem_limit_bytes=8 * MIB),
         name="finish",
-    )(scalars, gram, *basis)
+    )(table, gram, *basis)
 
 
 def on_device(positions, types, tile_lists, hardness, electroneg, gamma_table):
@@ -348,36 +361,24 @@
     edge = (atoms * VOLUME) ** (1.0 / 3.0) / CUTOFF
     box = tile_lists // TILES
     place = (box % 3) * 9 + box // 3 % 3 * 3 + box // 9
-    lists = place * TILES + tile_lists % TILES
     rows = place * 2 * TILES + tile_lists % TILES
     inside = jnp.ones((27,), bool)
     for k, axis in enumerate(AXES):
         there = lax.axis_index(axis) + OFFSETS[:, k].astype(np.int32)
         inside = inside & (there >= 0) & (there < lax.axis_size(axis))
     far = jnp.where(inside, 0.0, FAR).astype(F32)
-    powers = gamma_table**-1.5 * CUTOFF**-1.5
-    least, most = jnp.min(hardness), jnp.max(hardness)
-    centre = 0.5 * (least + most) + 1.0
-    spread = 0.5 * (most - least) + 1.5
-    scale = 20.0 * COULOMB / CUTOFF
-    scalars = jnp.concatenate(
-        [
-            jnp.stack([scale / spread, 1.0 / spread]),
-            (hardness - centre) / spread,
-            jnp.stack([spread, centre]),
-        ]
-    )
+    table = jnp.concatenate([hardness, electroneg, gamma_table])
     kinds = types.reshape(TILES, W).astype(F32)
     cells = jnp.concatenate([positions.reshape(3 * TILES, W), kinds], axis=0)
     near = surrounded(cells)
-    blocks, start = build(lists, far, powers, electroneg, near, edge)
+    blocks, start = build(rows, far, table, near, edge)
     basis = [start[16 * HOME : 16 * HOME + 16]]
     around = start
     for _ in range(ITERS - 1):
-        basis.append(product(rows, scalars, around, kinds, blocks))
+        basis.append(product(rows, table, around, kinds, blocks))
         around = surrounded(basis[-1]).reshape(27 * 16, W)
-    gram = summed(product(rows, scalars, around, kinds, blocks, tuple(basis[:-1])))
-    charges, solutions = finish(scalars, gram, basis)
+    gram = summed(product(rows, table, around, kinds, blocks, tuple(basis[:-1])))
+    charges, solutions = finish(table, gram, basis)
     solutions = jnp.transpose(solutions, (1, 0, 2)).reshape(1, 1, 1, 2, atoms)
     return charges.reshape(1, 1, 1, atoms), solutions
 

time: 153 us -> 149 us (0.974)
  between operations: 3.68 us -> 0.95 us
  other arithmetic: 7.55 us -> 5.03 us
    ppermute x12, waiting for transfers between devices: 4.44 us -> 6.74 us  [surrounded(): lax.ppermute(cells, axis, [((i + 1) % count, i) for i in range(count)])]
    ppermute x12, starting transfers between devices: 9.02 us -> 10.6 us  [surrounded(): lax.ppermute(cells, axis, [(i, (i + 1) % count) for i in range(count)])]
  transfers between devices with their start and end apart: 35 -> 35, of which waited for: 25 -> 27; matrix products, arithmetic and copies ran while one was open for 4% -> 3% of each run, Pallas kernels for 0% -> 0%
where the time goes in v3:
time: 149 us
  starting transfers between devices  59.5 us (40%)
  waiting for transfers between devices  44.9 us (30%)
  Pallas kernels  38.1 us (26%)
  other arithmetic  5.03 us (3%)
    ppermute x12, starting transfers between devices, surrounded(): lax.ppermute(cells, axis, [((i + 1) % count, i) for i in range(count)])  31.2 us
    ppermute x12, waiting for transfers between devices, surrounded(): lax.ppermute(cells, axis, [(i, (i + 1) % count) for i in range(count)])  22.2 us
    pallas_call x4, Pallas kernels, product(): pl.pallas_call(functools.partial(product_kernel, last), out_shape=jax.Sha...  19.6 us
    ppermute x11, starting transfers between devices, met(): lax.ppermute(rows, axis, [(i, i ^ step) for i in range(count)])  17.7 us
    pallas_call x1, Pallas kernels, build(): pl.pallas_call(functools.partial(build_kernel, edge), out_shape=(pltpu.VM...  16.1 us
    ppermute x11, waiting for transfers between devices, met(): lax.ppermute(rows, axis, [(i, i ^ step) for i in range(count)])  16 us
    ppermute x12, starting transfers between devices, surrounded(): lax.ppermute(cells, axis, [(i, (i + 1) % count) for i in range(count)])  10.6 us
    ppermute x12, waiting for transfers between devices, surrounded(): lax.ppermute(cells, axis, [((i + 1) % count, i) for i in range(count)])  6.74 us
  transfers between devices with their start and end apart: 35, of which 27 were waited for; matrix products, arithmetic and copies ran while one was open for 3% of the time, Pallas kernels for 0%

profile of v3, /device:TPU:16, one launch (start us, length us, event | category | flops | bytes accessed | tf_op | source)
XLA Modules:
  0.0 148.7 jit_solution(13423044881578966231)
XLA Ops:
  8.1 4.2 %collective-permute-start.3 = (f32[3,32,128]{2,1,0:T(8,128)S(1)}, f32[3,32,128]{2,1,0:T(8,128)S(1)}, u32[]{:S(2)}, u32[]{:S(2)}) collective-permute-start(f32[3,32,128]{2,1,0:T(8,128)S(1)} %pad_maximum_fusion), channel_id=1, source_target_pairs={{8,0},{16,8},{24,16},{32,24},{40,32},{48,40},{56,48},{0,56},{9,1},... | collective-permute-start | bytes 147464 | tf_op jit(solution)/shard_map/ppermute | solution.py:40
  14.4 2.0 %collective-permute-start.4 = (f32[9,32,128]{2,1,0:T(8,128)S(1)}, f32[9,32,128]{2,1,0:T(8,128)S(1)}, u32[]{:S(2)}, u32[]{:S(2)}) collective-permute-start(f32[9,32,128]{2,1,0:T(8,128)S(1)} %constant_dynamic-update-slice_fusion), channel_id=1, source_target_pairs={{0,1},{1,2},{2,3},{3,4},{4,5},{5,6},{6,7},{7,0},{8,9},{9,10},{10,1... | collective-permute-start | bytes 442376 | tf_op jit(solution)/shard_map/ppermute | solution.py:39
  17.8 4.0 %collective-permute-start.5 = (f32[9,32,128]{2,1,0:T(8,128)S(1)}, f32[9,32,128]{2,1,0:T(8,128)S(1)}, u32[]{:S(2)}, u32[]{:S(2)}) collective-permute-start(f32[9,32,128]{2,1,0:T(8,128)S(1)} %constant_dynamic-update-slice_fusion), channel_id=1, source_target_pairs={{1,0},{2,1},{3,2},{4,3},{5,4},{6,5},{7,6},{0,7},{9,8},{10,9},{11,1... | collective-permute-start | bytes 442376 | tf_op jit(solution)/shard_map/ppermute | solution.py:40
  24.5 16.1 %build.1 = (f32[8,36,128,128]{3,2,1,0:T(8,128)S(1)}, f32[432,128]{1,0:T(8,128)S(1)}) custom-call(s32[8,36]{1,0:T(8,128)S(1)} %fusion.4.lists, f32[27]{0:T(128)S(1)} %and_select_fusion.far, f32[12]{0:T(128)S(1)} %pad_maximum_fusion.4.table, f32[27,32,128]{2,1,0:T(8,128)S(1)} %constant_dynamic-update-slice_fusion.5.near), custom_call_target="tpu_custom_call" | custom-call | tf_op jit(solution)/shard_map/build/pallas_call | solution.py:154
  40.6 4.8 %product.4.rest_1_.v1 = f32[16,128]{1,0:T(8,128)S(1)} custom-call(s32[8,36]{1,0:T(8,128)S(1)} %fusion.4.lists, f32[12]{0:T(128)S(1)} %pad_maximum_fusion.4.table, f32[432,128]{1,0:T(8,128)S(1)} %get-tuple-element.6.around, f32[8,128]{1,0:T(8,128)S(1)} %bitcast.36, f32[8,36,128,128]{3,2,1,0:T(8,128)S(1)} %get-tuple-element.7.blocks), custom_call_target="tpu_custom_call" | custom-call | tf_op jit(solution)/shard_map/product/pallas_call | solution.py:235
  46.9 1.8 %collective-permute-done.6 = f32[1,16,128]{2,1,0:T(8,128)S(1)} collective-permute-done((f32[1,16,128]{2,1,0:T(8,128)S(1)}, f32[1,16,128]{2,1,0:T(8,128)S(1)}, u32[]{:S(2)}, u32[]{:S(2)}) %collective-permute-start.6) | collective-permute-done | bytes 8224 | tf_op jit(solution)/shard_map/ppermute | solution.py:39
  48.7 5.6 %collective-permute-start.9 = (f32[3,16,128]{2,1,0:T(8,128)S(1)}, f32[3,16,128]{2,1,0:T(8,128)S(1)}, u32[]{:S(2)}, u32[]{:S(2)}) collective-permute-start(f32[3,16,128]{2,1,0:T(8,128)S(1)} %pad_maximum_fusion.1), channel_id=1, source_target_pairs={{8,0},{16,8},{24,16},{32,24},{40,32},{48,40},{56,48},{0,56},{9,1},... | collective-permute-start | bytes 73736 | tf_op jit(solution)/shard_map/ppermute | solution.py:40
  54.3 1.8 %collective-permute-done.8 = f32[3,16,128]{2,1,0:T(8,128)S(1)} collective-permute-done((f32[3,16,128]{2,1,0:T(8,128)S(1)}, f32[3,16,128]{2,1,0:T(8,128)S(1)}, u32[]{:S(2)}, u32[]{:S(2)}) %collective-permute-start.8) | collective-permute-done | bytes 24608 | tf_op jit(solution)/shard_map/ppermute | solution.py:39
  56.6 3.3 %collective-permute-start.11 = (f32[9,16,128]{2,1,0:T(8,128)S(1)}, f32[9,16,128]{2,1,0:T(8,128)S(1)}, u32[]{:S(2)}, u32[]{:S(2)}) collective-permute-start(f32[9,16,128]{2,1,0:T(8,128)S(1)} %constant_dynamic-update-slice_fusion.12), channel_id=1, source_target_pairs={{1,0},{2,1},{3,2},{4,3},{5,4},{6,5},{7,6},{0,7},{9,8},{10,9},{11,1... | collective-permute-start | bytes 221192 | tf_op jit(solution)/shard_map/ppermute | solution.py:40
  60.0 2.2 %collective-permute-done.10 = f32[9,16,128]{2,1,0:T(8,128)S(1)} collective-permute-done((f32[9,16,128]{2,1,0:T(8,128)S(1)}, f32[9,16,128]{2,1,0:T(8,128)S(1)}, u32[]{:S(2)}, u32[]{:S(2)}) %collective-permute-start.10) | collective-permute-done | bytes 73760 | tf_op jit(solution)/shard_map/ppermute | solution.py:39
  62.3 4.8 %product.5.rest_2_.v2 = f32[16,128]{1,0:T(8,128)S(1)} custom-call(s32[8,36]{1,0:T(8,128)S(1)} %fusion.4.lists, f32[12]{0:T(128)S(1)} %pad_maximum_fusion.4.table, f32[432,128]{1,0:T(8,128)S(1)} %bitcast.24, f32[8,128]{1,0:T(8,128)S(1)} %bitcast.37, f32[8,36,128,128]{3,2,1,0:T(8,128)S(1)} %get-tuple-element.7.blocks), custom_call_target="tpu_custom_call" | custom-call | tf_op jit(solution)/shard_map/product/pallas_call | solution.py:235
  68.8 1.8 %collective-permute-done.12 = f32[1,16,128]{2,1,0:T(8,128)S(1)} collective-permute-done((f32[1,16,128]{2,1,0:T(8,128)S(1)}, f32[1,16,128]{2,1,0:T(8,128)S(1)}, u32[]{:S(2)}, u32[]{:S(2)}) %collective-permute-start.12) | collective-permute-done | bytes 8224 | tf_op jit(solution)/shard_map/ppermute | solution.py:39
  70.6 5.6 %collective-permute-start.15 = (f32[3,16,128]{2,1,0:T(8,128)S(1)}, f32[3,16,128]{2,1,0:T(8,128)S(1)}, u32[]{:S(2)}, u32[]{:S(2)}) collective-permute-start(f32[3,16,128]{2,1,0:T(8,128)S(1)} %pad_maximum_fusion.2), channel_id=1, source_target_pairs={{8,0},{16,8},{24,16},{32,24},{40,32},{48,40},{56,48},{0,56},{9,1},... | collective-permute-start | bytes 73736 | tf_op jit(solution)/shard_map/ppermute | solution.py:40
  76.2 1.8 %collective-permute-done.14 = f32[3,16,128]{2,1,0:T(8,128)S(1)} collective-permute-done((f32[3,16,128]{2,1,0:T(8,128)S(1)}, f32[3,16,128]{2,1,0:T(8,128)S(1)}, u32[]{:S(2)}, u32[]{:S(2)}) %collective-permute-start.14) | collective-permute-done | bytes 24608 | tf_op jit(solution)/shard_map/ppermute | solution.py:39
  78.1 3.0 %collective-permute-start.16 = (f32[9,16,128]{2,1,0:T(8,128)S(1)}, f32[9,16,128]{2,1,0:T(8,128)S(1)}, u32[]{:S(2)}, u32[]{:S(2)}) collective-permute-start(f32[9,16,128]{2,1,0:T(8,128)S(1)} %constant_dynamic-update-slice_fusion.24), channel_id=1, source_target_pairs={{0,1},{1,2},{2,3},{3,4},{4,5},{5,6},{6,7},{7,0},{8,9},{9,10},{10,1... | collective-permute-start | bytes 221192 | tf_op jit(solution)/shard_map/ppermute | solution.py:39
  81.5 2.2 %collective-permute-done.16 = f32[9,16,128]{2,1,0:T(8,128)S(1)} collective-permute-done((f32[9,16,128]{2,1,0:T(8,128)S(1)}, f32[9,16,128]{2,1,0:T(8,128)S(1)}, u32[]{:S(2)}, u32[]{:S(2)}) %collective-permute-start.16) | collective-permute-done | bytes 73760 | tf_op jit(solution)/shard_map/ppermute | solution.py:39
  85.4 4.8 %product.6.v3 = f32[16,128]{1,0:T(8,128)S(1)} custom-call(s32[8,36]{1,0:T(8,128)S(1)} %fusion.4.lists, f32[12]{0:T(128)S(1)} %pad_maximum_fusion.4.table, f32[432,128]{1,0:T(8,128)S(1)} %bitcast.25, f32[8,128]{1,0:T(8,128)S(1)} %bitcast.38, f32[8,36,128,128]{3,2,1,0:T(8,128)S(1)} %get-tuple-element.7.blocks), custom_call_target="tpu_custom_call" | custom-call | tf_op jit(solution)/shard_map/product/pallas_call | solution.py:235
  91.7 1.8 %collective-permute-done.18 = f32[1,16,128]{2,1,0:T(8,128)S(1)} collective-permute-done((f32[1,16,128]{2,1,0:T(8,128)S(1)}, f32[1,16,128]{2,1,0:T(8,128)S(1)}, u32[]{:S(2)}, u32[]{:S(2)}) %collective-permute-start.18) | collective-permute-done | bytes 8224 | tf_op jit(solution)/shard_map/ppermute | solution.py:39
  93.5 5.6 %collective-permute-start.21 = (f32[3,16,128]{2,1,0:T(8,128)S(1)}, f32[3,16,128]{2,1,0:T(8,128)S(1)}, u32[]{:S(2)}, u32[]{:S(2)}) collective-permute-start(f32[3,16,128]{2,1,0:T(8,128)S(1)} %pad_maximum_fusion.3), channel_id=1, source_target_pairs={{8,0},{16,8},{24,16},{32,24},{40,32},{48,40},{56,48},{0,56},{9,1},... | collective-permute-start | bytes 73736 | tf_op jit(solution)/shard_map/ppermute | solution.py:40
  99.2 1.8 %collective-permute-done.20 = f32[3,16,128]{2,1,0:T(8,128)S(1)} collective-permute-done((f32[3,16,128]{2,1,0:T(8,128)S(1)}, f32[3,16,128]{2,1,0:T(8,128)S(1)}, u32[]{:S(2)}, u32[]{:S(2)}) %collective-permute-start.20) | collective-permute-done | bytes 24608 | tf_op jit(solution)/shard_map/ppermute | solution.py:39
  101.0 2.1 %collective-permute-start.22 = (f32[9,16,128]{2,1,0:T(8,128)S(1)}, f32[9,16,128]{2,1,0:T(8,128)S(1)}, u32[]{:S(2)}, u32[]{:S(2)}) collective-permute-start(f32[9,16,128]{2,1,0:T(8,128)S(1)} %constant_dynamic-update-slice_fusion.36), channel_id=1, source_target_pairs={{0,1},{1,2},{2,3},{3,4},{4,5},{5,6},{6,7},{7,0},{8,9},{9,10},{10,1... | collective-permute-start | bytes 221192 | tf_op jit(solution)/shard_map/ppermute | solution.py:39
  104.3 2.3 %collective-permute-done.22 = f32[9,16,128]{2,1,0:T(8,128)S(1)} collective-permute-done((f32[9,16,128]{2,1,0:T(8,128)S(1)}, f32[9,16,128]{2,1,0:T(8,128)S(1)}, u32[]{:S(2)}, u32[]{:S(2)}) %collective-permute-start.22) | collective-permute-done | bytes 73760 | tf_op jit(solution)/shard_map/ppermute | solution.py:39
  107.5 5.1 %product.7 = f32[8,128]{1,0:T(8,128)S(1)} custom-call(s32[8,36]{1,0:T(8,128)S(1)} %fusion.4.lists, f32[12]{0:T(128)S(1)} %pad_maximum_fusion.4.table, f32[432,128]{1,0:T(8,128)S(1)} %bitcast.26, f32[8,128]{1,0:T(8,128)S(1)} %bitcast.39, f32[8,36,128,128]{3,2,1,0:T(8,128)S(1)} %get-tuple-element.7.blocks, f32[16,128]{1,0:T(8,128)S(1)} %slice.3.rest_0_.v0, ...), custom_call_target="tpu_custom_call" | custom-call | tf_op jit(solution)/shard_map/product/pallas_call | solution.py:235
  113.8 1.8 %collective-permute-start.26 = (f32[8,128]{1,0:T(8,128)S(1)}, f32[8,128]{1,0:T(8,128)S(1)}, u32[]{:S(2)}, u32[]{:S(2)}) collective-permute-start(f32[8,128]{1,0:T(8,128)S(1)} %add.97), channel_id=1, source_target_pairs={{0,128},{32,160},{128,0},{160,32},{1,129},{33,161},{129,1},{161,33... | collective-permute-start | bytes 12296 | tf_op jit(solution)/shard_map/ppermute | solution.py:47
  117.4 3.3 %collective-permute-done.25 = f32[8,128]{1,0:T(8,128)S(1)} collective-permute-done((f32[8,128]{1,0:T(8,128)S(1)}, f32[8,128]{1,0:T(8,128)S(1)}, u32[]{:S(2)}, u32[]{:S(2)}) %collective-permute-start.25) | collective-permute-done | bytes 4128 | tf_op jit(solution)/shard_map/ppermute | solution.py:47
  120.7 5.5 %collective-permute-start.30 = (f32[8,128]{1,0:T(8,128)S(1)}, f32[8,128]{1,0:T(8,128)S(1)}, u32[]{:S(2)}, u32[]{:S(2)}) collective-permute-start(f32[8,128]{1,0:T(8,128)S(1)} %add_add_fusion.2), channel_id=1, source_target_pairs={{0,24},{8,16},{16,8},{24,0},{1,25},{9,17},{17,9},{25,1},{2,26},{10... | collective-permute-start | bytes 12296 | tf_op jit(solution)/shard_map/ppermute | solution.py:47
  127.8 3.5 %collective-permute-done.29 = f32[8,128]{1,0:T(8,128)S(1)} collective-permute-done((f32[8,128]{1,0:T(8,128)S(1)}, f32[8,128]{1,0:T(8,128)S(1)}, u32[]{:S(2)}, u32[]{:S(2)}) %collective-permute-start.29) | collective-permute-done | bytes 4128 | tf_op jit(solution)/shard_map/ppermute | solution.py:47
  131.3 2.8 %collective-permute-start.33 = (f32[8,128]{1,0:T(8,128)S(1)}, f32[8,128]{1,0:T(8,128)S(1)}, u32[]{:S(2)}, u32[]{:S(2)}) collective-permute-start(f32[8,128]{1,0:T(8,128)S(1)} %add_add_fusion.1), channel_id=1, source_target_pairs={{0,3},{1,2},{2,1},{3,0},{4,7},{5,6},{6,5},{7,4},{8,11},{9,10},{10,... | collective-permute-start | bytes 12296 | tf_op jit(solution)/shard_map/ppermute | solution.py:47
  136.8 1.9 %collective-permute-done.32 = f32[8,128]{1,0:T(8,128)S(1)} collective-permute-done((f32[8,128]{1,0:T(8,128)S(1)}, f32[8,128]{1,0:T(8,128)S(1)}, u32[]{:S(2)}, u32[]{:S(2)}) %collective-permute-start.32) | collective-permute-done | bytes 4128 | tf_op jit(solution)/shard_map/ppermute | solution.py:47
  138.7 3.0 %collective-permute-start.34 = (f32[8,128]{1,0:T(8,128)S(1)}, f32[8,128]{1,0:T(8,128)S(1)}, u32[]{:S(2)}, u32[]{:S(2)}) collective-permute-start(f32[8,128]{1,0:T(8,128)S(1)} %add_add_fusion), channel_id=1, source_target_pairs={{0,4},{1,5},{2,6},{3,7},{4,0},{5,1},{6,2},{7,3},{8,12},{9,13},{10,... | collective-permute-start | bytes 12296 | tf_op jit(solution)/shard_map/ppermute | solution.py:47
  141.7 4.6 %collective-permute-done.34 = f32[8,128]{1,0:T(8,128)S(1)} collective-permute-done((f32[8,128]{1,0:T(8,128)S(1)}, f32[8,128]{1,0:T(8,128)S(1)}, u32[]{:S(2)}, u32[]{:S(2)}) %collective-permute-start.34) | collective-permute-done | bytes 4128 | tf_op jit(solution)/shard_map/ppermute | solution.py:47
  146.3 2.4 %finish.1 = (f32[8,128]{1,0:T(8,128)}, f32[8,2,128]{2,1,0:T(2,128)}) custom-call(f32[12]{0:T(128)S(1)} %pad_maximum_fusion.4.table, f32[8,128]{1,0:T(8,128)S(1)} %add.107.gram, f32[16,128]{1,0:T(8,128)S(1)} %slice.3.rest_0_.v0, f32[16,128]{1,0:T(8,128)S(1)} %product.4.rest_1_.v1, f32[16,128]{1,0:T(8,128)S(1)} %product.5.rest_2_.v2, f32[16,128]{1,0:T(8,128)S(1)} %product.6.v3), custom_call_target="tpu_custom_call" | custom-call | tf_op jit(solution)/shard_map/finish/pallas_call | solution.py:349
  (107 shorter events, 30.1 us)
Async XLA Ops:
  2.0 2.2 %collective-permute-start.1 = (f32[1,32,128]{2,1,0:T(8,128)S(1)}, f32[1,32,128]{2,1,0:T(8,128)S(1)}, u32[]{:S(2)}, u32[]{:S(2)}) collective-permute-start(f32[1,32,128]{2,1,0:T(8,128)S(1)} %maximum_bitcast_fusion), channel_id=1, source_target_pairs={{64,0},{128,64},{192,128},{0,192},{65,1},{129,65},{193,129},{1,193... | collective-permute-start | bytes 49160 | tf_op jit(solution)/shard_map/ppermute | solution.py:40
  2.8 3.2 %collective-permute-start = (f32[1,32,128]{2,1,0:T(8,128)S(1)}, f32[1,32,128]{2,1,0:T(8,128)S(1)}, u32[]{:S(2)}, u32[]{:S(2)}) collective-permute-start(f32[1,32,128]{2,1,0:T(8,128)S(1)} %maximum_bitcast_fusion), channel_id=1, source_target_pairs={{0,64},{64,128},{128,192},{192,0},{1,65},{65,129},{129,193},{193,1... | collective-permute-start | bytes 49160 | tf_op jit(solution)/shard_map/ppermute | solution.py:39
  5.9 7.7 %collective-permute-start.2 = (f32[3,32,128]{2,1,0:T(8,128)S(1)}, f32[3,32,128]{2,1,0:T(8,128)S(1)}, u32[]{:S(2)}, u32[]{:S(2)}) collective-permute-start(f32[3,32,128]{2,1,0:T(8,128)S(1)} %pad_maximum_fusion), channel_id=1, source_target_pairs={{0,8},{8,16},{16,24},{24,32},{32,40},{40,48},{48,56},{56,0},{1,9},... | collective-permute-start | bytes 147464 | tf_op jit(solution)/shard_map/ppermute | solution.py:39
  8.1 6.2 %collective-permute-start.3 = (f32[3,32,128]{2,1,0:T(8,128)S(1)}, f32[3,32,128]{2,1,0:T(8,128)S(1)}, u32[]{:S(2)}, u32[]{:S(2)}) collective-permute-start(f32[3,32,128]{2,1,0:T(8,128)S(1)} %pad_maximum_fusion), channel_id=1, source_target_pairs={{8,0},{16,8},{24,16},{32,24},{40,32},{48,40},{56,48},{0,56},{9,1},... | collective-permute-start | bytes 147464 | tf_op jit(solution)/shard_map/ppermute | solution.py:40
  14.4 9.1 %collective-permute-start.4 = (f32[9,32,128]{2,1,0:T(8,128)S(1)}, f32[9,32,128]{2,1,0:T(8,128)S(1)}, u32[]{:S(2)}, u32[]{:S(2)}) collective-permute-start(f32[9,32,128]{2,1,0:T(8,128)S(1)} %constant_dynamic-update-slice_fusion), channel_id=1, source_target_pairs={{0,1},{1,2},{2,3},{3,4},{4,5},{5,6},{6,7},{7,0},{8,9},{9,10},{10,1... | collective-permute-start | bytes 442376 | tf_op jit(solution)/shard_map/ppermute | solution.py:39
  17.8 6.6 %collective-permute-start.5 = (f32[9,32,128]{2,1,0:T(8,128)S(1)}, f32[9,32,128]{2,1,0:T(8,128)S(1)}, u32[]{:S(2)}, u32[]{:S(2)}) collective-permute-start(f32[9,32,128]{2,1,0:T(8,128)S(1)} %constant_dynamic-update-slice_fusion), channel_id=1, source_target_pairs={{1,0},{2,1},{3,2},{4,3},{5,4},{6,5},{7,6},{0,7},{9,8},{10,9},{11,1... | collective-permute-start | bytes 442376 | tf_op jit(solution)/shard_map/ppermute | solution.py:40
  45.5 3.2 %collective-permute-start.6 = (f32[1,16,128]{2,1,0:T(8,128)S(1)}, f32[1,16,128]{2,1,0:T(8,128)S(1)}, u32[]{:S(2)}, u32[]{:S(2)}) collective-permute-start(f32[1,16,128]{2,1,0:T(8,128)S(1)} %bitcast.28), channel_id=1, source_target_pairs={{0,64},{64,128},{128,192},{192,0},{1,65},{65,129},{129,193},{193,1... | collective-permute-start | bytes 24584 | tf_op jit(solution)/shard_map/ppermute | solution.py:39
  48.7 7.4 %collective-permute-start.8 = (f32[3,16,128]{2,1,0:T(8,128)S(1)}, f32[3,16,128]{2,1,0:T(8,128)S(1)}, u32[]{:S(2)}, u32[]{:S(2)}) collective-permute-start(f32[3,16,128]{2,1,0:T(8,128)S(1)} %pad_maximum_fusion.1), channel_id=1, source_target_pairs={{0,8},{8,16},{16,24},{24,32},{32,40},{40,48},{48,56},{56,0},{1,9},... | collective-permute-start | bytes 73736 | tf_op jit(solution)/shard_map/ppermute | solution.py:39
  48.7 7.5 %collective-permute-start.9 = (f32[3,16,128]{2,1,0:T(8,128)S(1)}, f32[3,16,128]{2,1,0:T(8,128)S(1)}, u32[]{:S(2)}, u32[]{:S(2)}) collective-permute-start(f32[3,16,128]{2,1,0:T(8,128)S(1)} %pad_maximum_fusion.1), channel_id=1, source_target_pairs={{8,0},{16,8},{24,16},{32,24},{40,32},{48,40},{56,48},{0,56},{9,1},... | collective-permute-start | bytes 73736 | tf_op jit(solution)/shard_map/ppermute | solution.py:40
  56.1 6.1 %collective-permute-start.10 = (f32[9,16,128]{2,1,0:T(8,128)S(1)}, f32[9,16,128]{2,1,0:T(8,128)S(1)}, u32[]{:S(2)}, u32[]{:S(2)}) collective-permute-start(f32[9,16,128]{2,1,0:T(8,128)S(1)} %constant_dynamic-update-slice_fusion.12), channel_id=1, source_target_pairs={{0,1},{1,2},{2,3},{3,4},{4,5},{5,6},{6,7},{7,0},{8,9},{9,10},{10,1... | collective-permute-start | bytes 221192 | tf_op jit(solution)/shard_map/ppermute | solution.py:39
  56.6 5.6 %collective-permute-start.11 = (f32[9,16,128]{2,1,0:T(8,128)S(1)}, f32[9,16,128]{2,1,0:T(8,128)S(1)}, u32[]{:S(2)}, u32[]{:S(2)}) collective-permute-start(f32[9,16,128]{2,1,0:T(8,128)S(1)} %constant_dynamic-update-slice_fusion.12), channel_id=1, source_target_pairs={{1,0},{2,1},{3,2},{4,3},{5,4},{6,5},{7,6},{0,7},{9,8},{10,9},{11,1... | collective-permute-start | bytes 221192 | tf_op jit(solution)/shard_map/ppermute | solution.py:40
  67.1 1.6 %collective-permute-start.13 = (f32[1,16,128]{2,1,0:T(8,128)S(1)}, f32[1,16,128]{2,1,0:T(8,128)S(1)}, u32[]{:S(2)}, u32[]{:S(2)}) collective-permute-start(f32[1,16,128]{2,1,0:T(8,128)S(1)} %bitcast.30), channel_id=1, source_target_pairs={{64,0},{128,64},{192,128},{0,192},{65,1},{129,65},{193,129},{1,193... | collective-permute-start | bytes 24584 | tf_op jit(solution)/shard_map/ppermute | solution.py:40
  67.4 3.2 %collective-permute-start.12 = (f32[1,16,128]{2,1,0:T(8,128)S(1)}, f32[1,16,128]{2,1,0:T(8,128)S(1)}, u32[]{:S(2)}, u32[]{:S(2)}) collective-permute-start(f32[1,16,128]{2,1,0:T(8,128)S(1)} %bitcast.31), channel_id=1, source_target_pairs={{0,64},{64,128},{128,192},{192,0},{1,65},{65,129},{129,193},{193,1... | collective-permute-start | bytes 24584 | tf_op jit(solution)/shard_map/ppermute | solution.py:39
  70.6 7.4 %collective-permute-start.14 = (f32[3,16,128]{2,1,0:T(8,128)S(1)}, f32[3,16,128]{2,1,0:T(8,128)S(1)}, u32[]{:S(2)}, u32[]{:S(2)}) collective-permute-start(f32[3,16,128]{2,1,0:T(8,128)S(1)} %pad_maximum_fusion.2), channel_id=1, source_target_pairs={{0,8},{8,16},{16,24},{24,32},{32,40},{40,48},{48,56},{56,0},{1,9},... | collective-permute-start | bytes 73736 | tf_op jit(solution)/shard_map/ppermute | solution.py:39
  70.6 7.5 %collective-permute-start.15 = (f32[3,16,128]{2,1,0:T(8,128)S(1)}, f32[3,16,128]{2,1,0:T(8,128)S(1)}, u32[]{:S(2)}, u32[]{:S(2)}) collective-permute-start(f32[3,16,128]{2,1,0:T(8,128)S(1)} %pad_maximum_fusion.2), channel_id=1, source_target_pairs={{8,0},{16,8},{24,16},{32,24},{40,32},{48,40},{56,48},{0,56},{9,1},... | collective-permute-start | bytes 73736 | tf_op jit(solution)/shard_map/ppermute | solution.py:40
  78.1 5.6 %collective-permute-start.16 = (f32[9,16,128]{2,1,0:T(8,128)S(1)}, f32[9,16,128]{2,1,0:T(8,128)S(1)}, u32[]{:S(2)}, u32[]{:S(2)}) collective-permute-start(f32[9,16,128]{2,1,0:T(8,128)S(1)} %constant_dynamic-update-slice_fusion.24), channel_id=1, source_target_pairs={{0,1},{1,2},{2,3},{3,4},{4,5},{5,6},{6,7},{7,0},{8,9},{9,10},{10,1... | collective-permute-start | bytes 221192 | tf_op jit(solution)/shard_map/ppermute | solution.py:39
  81.1 4.4 %collective-permute-start.17 = (f32[9,16,128]{2,1,0:T(8,128)S(1)}, f32[9,16,128]{2,1,0:T(8,128)S(1)}, u32[]{:S(2)}, u32[]{:S(2)}) collective-permute-start(f32[9,16,128]{2,1,0:T(8,128)S(1)} %constant_dynamic-update-slice_fusion.24), channel_id=1, source_target_pairs={{1,0},{2,1},{3,2},{4,3},{5,4},{6,5},{7,6},{0,7},{9,8},{10,9},{11,1... | collective-permute-start | bytes 221192 | tf_op jit(solution)/shard_map/ppermute | solution.py:40
  90.4 3.2 %collective-permute-start.18 = (f32[1,16,128]{2,1,0:T(8,128)S(1)}, f32[1,16,128]{2,1,0:T(8,128)S(1)}, u32[]{:S(2)}, u32[]{:S(2)}) collective-permute-start(f32[1,16,128]{2,1,0:T(8,128)S(1)} %bitcast.41), channel_id=1, source_target_pairs={{0,64},{64,128},{128,192},{192,0},{1,65},{65,129},{129,193},{193,1... | collective-permute-start | bytes 24584 | tf_op jit(solution)/shard_map/ppermute | solution.py:39
  93.5 7.4 %collective-permute-start.20 = (f32[3,16,128]{2,1,0:T(8,128)S(1)}, f32[3,16,128]{2,1,0:T(8,128)S(1)}, u32[]{:S(2)}, u32[]{:S(2)}) collective-permute-start(f32[3,16,128]{2,1,0:T(8,128)S(1)} %pad_maximum_fusion.3), channel_id=1, source_target_pairs={{0,8},{8,16},{16,24},{24,32},{32,40},{40,48},{48,56},{56,0},{1,9},... | collective-permute-start | bytes 73736 | tf_op jit(solution)/shard_map/ppermute | solution.py:39
  93.5 7.5 %collective-permute-start.21 = (f32[3,16,128]{2,1,0:T(8,128)S(1)}, f32[3,16,128]{2,1,0:T(8,128)S(1)}, u32[]{:S(2)}, u32[]{:S(2)}) collective-permute-start(f32[3,16,128]{2,1,0:T(8,128)S(1)} %pad_maximum_fusion.3), channel_id=1, source_target_pairs={{8,0},{16,8},{24,16},{32,24},{40,32},{48,40},{56,48},{0,56},{9,1},... | collective-permute-start | bytes 73736 | tf_op jit(solution)/shard_map/ppermute | solution.py:40
  101.0 5.6 %collective-permute-start.22 = (f32[9,16,128]{2,1,0:T(8,128)S(1)}, f32[9,16,128]{2,1,0:T(8,128)S(1)}, u32[]{:S(2)}, u32[]{:S(2)}) collective-permute-start(f32[9,16,128]{2,1,0:T(8,128)S(1)} %constant_dynamic-update-slice_fusion.36), channel_id=1, source_target_pairs={{0,1},{1,2},{2,3},{3,4},{4,5},{5,6},{6,7},{7,0},{8,9},{9,10},{10,1... | collective-permute-start | bytes 221192 | tf_op jit(solution)/shard_map/ppermute | solution.py:39
  103.1 4.4 %collective-permute-start.23 = (f32[9,16,128]{2,1,0:T(8,128)S(1)}, f32[9,16,128]{2,1,0:T(8,128)S(1)}, u32[]{:S(2)}, u32[]{:S(2)}) collective-permute-start(f32[9,16,128]{2,1,0:T(8,128)S(1)} %constant_dynamic-update-slice_fusion.36), channel_id=1, source_target_pairs={{1,0},{2,1},{3,2},{4,3},{5,4},{6,5},{7,6},{0,7},{9,8},{10,9},{11,1... | collective-permute-start | bytes 221192 | tf_op jit(solution)/shard_map/ppermute | solution.py:40
  113.8 3.6 %collective-permute-start.27 = (f32[8,128]{1,0:T(8,128)S(1)}, f32[8,128]{1,0:T(8,128)S(1)}, u32[]{:S(2)}, u32[]{:S(2)}) collective-permute-start(f32[8,128]{1,0:T(8,128)S(1)} %add.97), channel_id=1, source_target_pairs={{0,160},{32,128},{128,32},{160,0},{1,161},{33,129},{129,33},{161,1... | collective-permute-start | bytes 12296 | tf_op jit(solution)/shard_map/ppermute | solution.py:47
  113.8 3.6 %collective-permute-start.26 = (f32[8,128]{1,0:T(8,128)S(1)}, f32[8,128]{1,0:T(8,128)S(1)}, u32[]{:S(2)}, u32[]{:S(2)}) collective-permute-start(f32[8,128]{1,0:T(8,128)S(1)} %add.97), channel_id=1, source_target_pairs={{0,128},{32,160},{128,0},{160,32},{1,129},{33,161},{129,1},{161,33... | collective-permute-start | bytes 12296 | tf_op jit(solution)/shard_map/ppermute | solution.py:47
  115.6 5.1 %collective-permute-start.25 = (f32[8,128]{1,0:T(8,128)S(1)}, f32[8,128]{1,0:T(8,128)S(1)}, u32[]{:S(2)}, u32[]{:S(2)}) collective-permute-start(f32[8,128]{1,0:T(8,128)S(1)} %add.97), channel_id=1, source_target_pairs={{0,32},{32,0},{128,160},{160,128},{1,33},{33,1},{129,161},{161,129... | collective-permute-start | bytes 12296 | tf_op jit(solution)/shard_map/ppermute | solution.py:47
  120.7 7.1 %collective-permute-start.30 = (f32[8,128]{1,0:T(8,128)S(1)}, f32[8,128]{1,0:T(8,128)S(1)}, u32[]{:S(2)}, u32[]{:S(2)}) collective-permute-start(f32[8,128]{1,0:T(8,128)S(1)} %add_add_fusion.2), channel_id=1, source_target_pairs={{0,24},{8,16},{16,8},{24,0},{1,25},{9,17},{17,9},{25,1},{2,26},{10... | collective-permute-start | bytes 12296 | tf_op jit(solution)/shard_map/ppermute | solution.py:47
  126.2 5.1 %collective-permute-start.29 = (f32[8,128]{1,0:T(8,128)S(1)}, f32[8,128]{1,0:T(8,128)S(1)}, u32[]{:S(2)}, u32[]{:S(2)}) collective-permute-start(f32[8,128]{1,0:T(8,128)S(1)} %add_add_fusion.2), channel_id=1, source_target_pairs={{0,16},{8,24},{16,0},{24,8},{1,17},{9,25},{17,1},{25,9},{2,18},{10... | collective-permute-start | bytes 12296 | tf_op jit(solution)/shard_map/ppermute | solution.py:47
  126.2 5.1 %collective-permute-start.28 = (f32[8,128]{1,0:T(8,128)S(1)}, f32[8,128]{1,0:T(8,128)S(1)}, u32[]{:S(2)}, u32[]{:S(2)}) collective-permute-start(f32[8,128]{1,0:T(8,128)S(1)} %add_add_fusion.2), channel_id=1, source_target_pairs={{0,8},{8,0},{16,24},{24,16},{1,9},{9,1},{17,25},{25,17},{2,10},{10... | collective-permute-start | bytes 12296 | tf_op jit(solution)/shard_map/ppermute | solution.py:47
  131.3 5.5 %collective-permute-start.33 = (f32[8,128]{1,0:T(8,128)S(1)}, f32[8,128]{1,0:T(8,128)S(1)}, u32[]{:S(2)}, u32[]{:S(2)}) collective-permute-start(f32[8,128]{1,0:T(8,128)S(1)} %add_add_fusion.1), channel_id=1, source_target_pairs={{0,3},{1,2},{2,1},{3,0},{4,7},{5,6},{6,5},{7,4},{8,11},{9,10},{10,... | collective-permute-start | bytes 12296 | tf_op jit(solution)/shard_map/ppermute | solution.py:47
  134.1 4.5 %collective-permute-start.32 = (f32[8,128]{1,0:T(8,128)S(1)}, f32[8,128]{1,0:T(8,128)S(1)}, u32[]{:S(2)}, u32[]{:S(2)}) collective-permute-start(f32[8,128]{1,0:T(8,128)S(1)} %add_add_fusion.1), channel_id=1, source_target_pairs={{0,2},{1,3},{2,0},{3,1},{4,6},{5,7},{6,4},{7,5},{8,10},{9,11},{10,... | collective-permute-start | bytes 12296 | tf_op jit(solution)/shard_map/ppermute | solution.py:47
  134.2 4.5 %collective-permute-start.31 = (f32[8,128]{1,0:T(8,128)S(1)}, f32[8,128]{1,0:T(8,128)S(1)}, u32[]{:S(2)}, u32[]{:S(2)}) collective-permute-start(f32[8,128]{1,0:T(8,128)S(1)} %add_add_fusion.1), channel_id=1, source_target_pairs={{0,1},{1,0},{2,3},{3,2},{4,5},{5,4},{6,7},{7,6},{8,9},{9,8},{10,11... | collective-permute-start | bytes 12296 | tf_op jit(solution)/shard_map/ppermute | solution.py:47
  138.7 7.6 %collective-permute-start.34 = (f32[8,128]{1,0:T(8,128)S(1)}, f32[8,128]{1,0:T(8,128)S(1)}, u32[]{:S(2)}, u32[]{:S(2)}) collective-permute-start(f32[8,128]{1,0:T(8,128)S(1)} %add_add_fusion), channel_id=1, source_target_pairs={{0,4},{1,5},{2,6},{3,7},{4,0},{5,1},{6,2},{7,3},{8,12},{9,13},{10,... | collective-permute-start | bytes 12296 | tf_op jit(solution)/shard_map/ppermute | solution.py:47
  (3 other events, 4.2 us)
